TPU v7x, 128 devices: a whole 4x4x4 slice. The times are simulated.
128 devices in a mesh: row: 16 (over x, z_hi, core), col: 8 (over y, z_lo).
Axes of the slice: x: 4, y: 4, z: 4 (z_hi: 2, z_lo: 2; z = z_hi * 2 + z_lo), core: 2. Of those that a mesh axis runs over, the one named last changes fastest.
Arguments:
- tile_values: bfloat16 [256, 8, 4, 128, 128], P(('row', 'col')), may hold values from 0 to 1
- tile_columns: int32 [256, 8, 4], P(('row', 'col')), may hold values from -1 to 255, as said below
- owner_map: int32 [256], replicated, may hold values from 0 to 255, as said below
- section_rows: int32 [2], replicated, may hold values from 0 to 15, as said below
Outputs:
- inflated: bfloat16 [32768, 12288], P('row', 'col')
Inputs may be any that keep to these rules, and one draw needn't show every extreme that they name: `tile_columns`: in each tile row and block-column b, the first 1 to 4 slots name distinct tile columns within b * 32 to b * 32 + 31 and the remaining slots hold -1; some tile row uses all 4 slots. A permutation of the tile rows; of the tile rows t in each aligned group of 16, exactly 1 have owner_map[t] in each block-row's range of 16 positions. `section_rows`: distinct block-rows; the last block-row is always one of them.
All inputs are finite; a program needn't handle non-finite values.
Results may differ from a plain program's by a relative error of at most 0.001.
Values may be sent and summed in bfloat16 or wider, within the bound.
A program may use at most 128 MiB of HBM per device.

v0:
```python
import jax
import jax.numpy as jnp
from jax import lax
from jax.sharding import Mesh
from jax.sharding import PartitionSpec as P

TILE = 128
SLAB = 12
SECTIONS = 2
ROW = ("row_0", "row_1", "row_2")
ROW_COL = ("row_0", "row_1", "row_2", "col")


def cut_along(x, dim, peers):
    dims = x.shape
    tiles = x.reshape(*dims[:dim], peers, dims[dim] // peers, *dims[dim + 1 :])
    return jnp.moveaxis(tiles, dim, 0)


def joined_along(tiles, dim):
    dims = list(tiles.shape[1:])
    dims[dim] *= tiles.shape[0]
    return jnp.moveaxis(tiles, 0, dim).reshape(dims)


def moved_by_axis(tiles, axes, turns):
    inside = tiles.shape[1:]
    out = tiles.reshape(*(lax.axis_size(a) for a in axes), *inside)
    for k in turns:
        out = lax.all_to_all(out, axes[k], k, k, tiled=True)
    return out.reshape(-1, *inside)


def two_step_exchange(x, groups, turns, split_dim, concat_dim):
    peers = lax.axis_size(groups[0]) * lax.axis_size(groups[1])
    tiles = cut_along(x, split_dim, peers)
    return joined_along(moved_by_axis(tiles, groups, turns), concat_dim)


def broadcast(x, axis, root):
    mine = lax.axis_index(axis) == root
    return lax.psum(jnp.where(mine, x, jnp.zeros_like(x)), axis)


def copy_for_each(x, axis):
    peers = lax.axis_size(axis)
    return lax.all_to_all(jnp.broadcast_to(x[None], (peers, *x.shape)), axis, 0, 0, tiled=True)


def over_copies(x, axis):
    return copy_for_each(x, axis).sum(axis=0)


def densify(values_in, columns_in, first_col):
    relative = columns_in - first_col
    picker = (relative[..., None] == jnp.arange(SLAB, dtype=jnp.int32)).astype(jnp.bfloat16)
    spread = jnp.einsum("nkab,nkj->najb", values_in, picker, preferred_element_type=jnp.float32)
    return spread.astype(jnp.bfloat16).reshape(values_in.shape[0], TILE, SLAB * TILE)


def per_device(tile_values, tile_columns, owner_map, section_rows):
    n_row = lax.axis_size(ROW)
    n_col = lax.axis_size("col")
    row_id = lax.axis_index(ROW)
    col_id = lax.axis_index("col")
    tile_count = owner_map.shape[0]
    rows_block = tile_values.shape[0] * n_col
    cols_block = tile_values.shape[0] * n_row
    first_col = col_id * cols_block
    every_columns = lax.all_gather(tile_columns, ROW_COL, axis=0, tiled=True)
    every_tile = jnp.arange(tile_count, dtype=jnp.int32)
    inverse = jnp.zeros((tile_count,), jnp.int32).at[owner_map].set(every_tile)
    grid_columns = every_columns[inverse]

    def block_lists(block_row, block_col):
        rows_part = lax.dynamic_slice_in_dim(grid_columns, block_row * rows_block, rows_block, 0)
        return jnp.take(rows_part, block_col, axis=1)

    spread_vals = lax.all_to_all(tile_values, "col", split_axis=1, concat_axis=0, tiled=True)
    spread_vals = spread_vals[:, 0]
    local_rows = jnp.arange(rows_block, dtype=jnp.int32)
    source_tiles = row_id * rows_block + local_rows
    target_block = owner_map[source_tiles] // rows_block
    send_order = jnp.argsort(target_block * rows_block + local_rows)
    recv_vals = two_step_exchange(
        spread_vals[send_order], (("row_0", "row_1"), "row_2"), (1, 0), 0, 0
    )
    owned = owner_map // rows_block == row_id
    arrived = jnp.argsort(jnp.where(owned, every_tile, every_tile + tile_count))[:rows_block]
    new_local = owner_map[arrived] - row_id * rows_block
    placed = jnp.argsort(new_local)
    block_vals = recv_vals[placed]
    slot_values = []
    slot_targets = []
    panels = []
    for section in range(SECTIONS):
        section_row = section_rows[section]
        source_col = section_row * n_col // n_row
        panel_vals = broadcast(block_vals, "col", source_col)
        panel_cols = block_lists(row_id, source_col)
        list_vals = broadcast(block_vals, ROW, section_row)
        panel_dense = densify(list_vals, block_lists(section_row, col_id), first_col)
        relative = panel_cols - section_row * rows_block
        inside = (relative >= 0) & (relative < rows_block)
        slot_targets.append(jnp.where(inside, relative, 0) + section * rows_block)
        slot_values.append(panel_vals * inside[..., None, None].astype(jnp.bfloat16))
        panels.append(panel_dense)
    all_values = jnp.concatenate(slot_values, axis=1)
    all_targets = jnp.concatenate(slot_targets, axis=1)
    all_panels = jnp.concatenate(panels, axis=0).reshape(SECTIONS * rows_block * TILE, SLAB * TILE)
    inner_count = SECTIONS * rows_block
    left_picker = (all_targets[..., None] == jnp.arange(inner_count, dtype=jnp.int32)).astype(
        jnp.bfloat16
    )
    left_dense = jnp.einsum(
        "nkab,nkj->najb", all_values, left_picker, preferred_element_type=jnp.float32
    )
    left_dense = left_dense.astype(jnp.bfloat16).reshape(rows_block * TILE, inner_count * TILE)
    expanded = jnp.dot(left_dense, all_panels, preferred_element_type=jnp.float32)
    squares = expanded * expanded
    column_part = jnp.sum(squares, axis=0)
    column_total = over_copies(column_part, ROW)
    factor = tile_count * TILE / (column_total + 1e-06)
    return (squares * factor).astype(jnp.bfloat16)


def solution(mesh):
    split = Mesh(
        mesh.devices.reshape(4, 2, 2, mesh.shape["col"]), ("row_0", "row_1", "row_2", "col")
    )
    in_specs = (P(ROW_COL, None, None, None, None), P(ROW_COL, None, None), P(), P())
    out_specs = P(ROW, "col")
    return jax.shard_map(
        per_device, mesh=split, in_specs=in_specs, out_specs=out_specs, check_vma=False
    )
```

profile of v0, /device:TPU:1, one launch (start us, length us, event | category | flops | bytes accessed | tf_op | source)
XLA Modules:
  0.0 567.8 jit_solution(13753688839111758612)
XLA Ops:
  6.5 3.2 copy.88
  9.7 6.5 %all-to-all-start = ((bf16[2,8,4,128,128]{4,3,2,0,1:T(8,128)(2,1)}), bf16[2,8,4,128,128]{4,3,2,0,1:T(8,128)(2,1)S(1)}, u32[]{:S(2)}, u32[]{:S(2)}) async-start(bf16[2,8,4,128,128]{4,3,2,0,1:T(8,128)(2,1)} %copy.88), calls=%async_computation | async-start | bytes 4194304 | tf_op jit(solution)/shard_map/all_to_all | solution.py:79
  16.9 3.2 sort.49
  21.5 25.3 %all-to-all-done = bf16[2,8,4,128,128]{4,3,2,0,1:T(8,128)(2,1)S(1)} async-done(((bf16[2,8,4,128,128]{4,3,2,0,1:T(8,128)(2,1)}), bf16[2,8,4,128,128]{4,3,2,0,1:T(8,128)(2,1)S(1)}, u32[]{:S(2)}, u32[]{:S(2)}) %all-to-all-start) | async-done | bytes 2097184 | tf_op jit(solution)/shard_map/all_to_all | solution.py:79
  46.8 2.1 gather_fusion.2
  48.9 1.7 copy.89
  50.7 6.6 %all_to_all.31 = bf16[8,2,1,4,128,128]{5,4,3,0,2,1:T(8,128)(2,1)S(1)} all-to-all(bf16[8,2,1,4,128,128]{5,4,3,0,2,1:T(8,128)(2,1)S(1)} %copy.89), channel_id=1, replica_groups=mesh['row_0'=4,'row_1'=2,'row_2'=2,'col'=8] {'row_2'}, dimensions={1} | all-to-all | bytes 4194304 | tf_op jit(solution)/shard_map/all_to_all | solution.py:30
  58.7 7.2 %all-to-all-start.2 = ((bf16[8,2,1,4,128,128]{5,4,3,1,2,0:T(8,128)(2,1)}), bf16[8,2,1,4,128,128]{5,4,3,1,2,0:T(8,128)(2,1)S(1)}, u32[]{:S(2)}, u32[]{:S(2)}) async-start(bf16[8,2,1,4,128,128]{5,4,3,1,2,0:T(8,128)(2,1)} %copy.90), calls=%async_computation.2 | async-start | bytes 4194304 | tf_op jit(solution)/shard_map/all_to_all | solution.py:30
  71.1 25.7 %all-to-all-done.2 = bf16[8,2,1,4,128,128]{5,4,3,1,2,0:T(8,128)(2,1)S(1)} async-done(((bf16[8,2,1,4,128,128]{5,4,3,1,2,0:T(8,128)(2,1)}), bf16[8,2,1,4,128,128]{5,4,3,1,2,0:T(8,128)(2,1)S(1)}, u32[]{:S(2)}, u32[]{:S(2)}) %all-to-all-start.2) | async-done | bytes 2097184 | tf_op jit(solution)/shard_map/all_to_all | solution.py:30
  96.8 2.1 gather_fusion.4
  99.0 7.6 %broadcast_select_fusion.3 = (bf16[16,4,128,128]{3,1,2,0:T(4,128)(2,1)}, bf16[16,4,128,128]{3,1,2,0:T(4,128)(2,1)}, bf16[16,4,128,128]{3,1,2,0:T(4,128)(2,1)}, bf16[16,4,128,128]{3,1,2,0:T(4,128)(2,1)}) fusion(pred[]{:T(512)S(6)} %eq.60, bf16[16,4,128,128]{3,2,1,0:T(8,128)(2,1)} %gather_fusion.4, pred[]{:T(512)S(6)} %eq.63, pred[]{:T(512)S(6)} %eq.67, ...), kind=kLoop, calls=%fused_computation.21 | loop fusion | flops 4194304 | bytes 10485764 | tf_op jit(solution)/shard_map/jit(_where)/select_n | solution.py:42
  110.1 301.1 %all_gather.3 = s32[256,8,4]{1,2,0:T(4,128)S(1)} all-gather(s32[2,8,4]{1,2,0:T(4,128)S(1)} %copy-done.3), channel_id=1, replica_groups=mesh['row_0'=4,'row_1'=2,'row_2'=2,'col'=8] {'row_0','row_1','row_2','col'}, dimensions={0}, use_global_device_ids=true | all-gather | bytes 33024 | tf_op jit(solution)/shard_map/all_gather | solution.py:70
  413.2 7.1 %convert_bitcast_fusion = bf16[16,128,12,128]{3,2,1,0:T(8,128)(2,1)} fusion(bf16[16,4,128,128]{3,1,2,0:T(4,128)(2,1)} %get-tuple-element.23, s32[16,4]{1,0:T(8,128)S(1)} %copy.100), kind=kOutput, calls=%fused_computation.13 | convolution fusion | flops 28312320 | bytes 8388864 | tf_op jit(solution)/shard_map/nkab,nkj->najb/dot_general | solution.py:57
  420.4 12.2 %copy.102 = bf16[16,128,12,128]{1,3,2,0:T(8,128)(2,1)} copy(bf16[16,128,12,128]{3,2,1,0:T(8,128)(2,1)} %convert_bitcast_fusion) | data formatting | bytes 12582912 | tf_op jit(solution)/shard_map/convert_element_type | solution.py:58
  432.6 6.4 %convert_bitcast_fusion.1 = bf16[16,128,12,128]{3,2,1,0:T(8,128)(2,1)} fusion(bf16[16,4,128,128]{3,1,2,0:T(4,128)(2,1)S(1)} %copy-done.1, s32[16,4]{1,0:T(8,128)S(1)} %copy.96), kind=kOutput, calls=%fused_computation.14 | convolution fusion | flops 28312320 | bytes 8388864 | tf_op jit(solution)/shard_map/nkab,nkj->najb/dot_general | solution.py:57
  439.0 12.0 %copy.98 = bf16[16,128,12,128]{1,3,2,0:T(8,128)(2,1)} copy(bf16[16,128,12,128]{3,2,1,0:T(8,128)(2,1)} %convert_bitcast_fusion.1) | data formatting | bytes 12582912 | tf_op jit(solution)/shard_map/convert_element_type | solution.py:58
  451.0 10.5 %pad_maximum_fusion = bf16[32,128,1536]{1,2,0:T(8,128)(2,1)} fusion(bf16[16,128,1536]{1,2,0:T(8,128)(2,1)} %bitcast.70, bf16[16,128,1536]{1,2,0:T(8,128)(2,1)} %bitcast.71), kind=kLoop, calls=%fused_computation.9 | loop fusion | flops 6291456 | bytes 25165824 | tf_op jit(solution)/shard_map/concatenate | solution.py:110
  461.5 16.6 %copy.103 = bf16[32,128,1536]{2,1,0:T(8,128)(2,1)} copy(bf16[32,128,1536]{1,2,0:T(8,128)(2,1)} %pad_maximum_fusion) | data formatting | bytes 25165824 | tf_op jit(solution)/shard_map/concatenate | solution.py:110
  478.1 4.0 broadcast_multiply_fusion
  482.1 2.3 broadcast_multiply_fusion.1
  484.4 9.9 %convolution_convert_fusion = bf16[16,32,128,128]{3,1,2,0:T(8,128)(2,1)} fusion(bf16[16,4,128,128]{3,1,2,0:T(4,128)(2,1)} %broadcast_multiply_fusion, bf16[16,4,128,128]{3,1,2,0:T(4,128)(2,1)} %broadcast_multiply_fusion.1, s32[16,8]{1,0:T(8,128)S(1)} %copy.87), kind=kOutput, calls=%fused_computation.12 | convolution fusion | flops 150999040 | bytes 20972032 | tf_op jit(solution)/shard_map/nkab,nkj->najb/dot_general | solution.py:115
  494.3 31.4 %multiply_reduce_fusion = (f32[1536]{0:T(1024)S(1)}, f32[2048,1536]{1,0:T(8,128)}) fusion(bf16[4096,1536]{1,0:T(8,128)(2,1)S(1)} %bitcast.74, bf16[256,8,32,128]{3,2,1,0:T(8,128)(2,1)} %bitcast.69), kind=kOutput, calls=%fused_computation.11 | convolution fusion | flops 25776093184 | bytes 41949184 | tf_op jit(solution)/shard_map/dot_general | solution.py:119
  525.8 26.1 %all_to_all.32 = f32[16,1,1536]{2,1,0:T(1,128)S(1)} all-to-all(f32[16,1,1536]{2,1,0:T(1,128)S(1)} %broadcast_in_dim.48), channel_id=1, replica_groups=mesh['row_0'=4,'row_1'=2,'row_2'=2,'col'=8] {'row_0','row_1','row_2'}, dimensions={0} | all-to-all | bytes 196608 | tf_op jit(solution)/shard_map/all_to_all | solution.py:47
  551.9 9.0 %multiply_convert_fusion = bf16[2048,1536]{1,0:T(8,128)(2,1)} fusion(f32[2048,1536]{1,0:T(8,128)} %get-tuple-element.40, f32[1536]{0:T(1024)S(1)} %add_divide_fusion), kind=kLoop, calls=%fused_computation.10 | loop fusion | flops 9437184 | bytes 18880512 | tf_op jit(solution)/shard_map/convert_element_type | solution.py:124
  (65 shorter events, 10.5 us)
Async XLA Ops:
  9.7 6.5 %copy-start = (s32[256]{0:T(256)S(1)}, s32[256]{0:T(256)}, u32[]{:S(2)}) copy-start(s32[256]{0:T(256)} %param.8) | copy-start | bytes 3076
  9.7 37.1 %all-to-all-start = ((bf16[2,8,4,128,128]{4,3,2,0,1:T(8,128)(2,1)}), bf16[2,8,4,128,128]{4,3,2,0,1:T(8,128)(2,1)S(1)}, u32[]{:S(2)}, u32[]{:S(2)}) async-start(bf16[2,8,4,128,128]{4,3,2,0,1:T(8,128)(2,1)} %copy.88), calls=%async_computation | async-start | bytes 4194304 | tf_op jit(solution)/shard_map/all_to_all | solution.py:79
  58.7 7.2 %copy-start.4 = (s32[2]{0:T(128)S(1)}, s32[2]{0:T(128)}, u32[]{:S(2)}) copy-start(s32[2]{0:T(128)} %param.9) | copy-start | bytes 28
  58.7 38.1 %all-to-all-start.2 = ((bf16[8,2,1,4,128,128]{5,4,3,1,2,0:T(8,128)(2,1)}), bf16[8,2,1,4,128,128]{5,4,3,1,2,0:T(8,128)(2,1)S(1)}, u32[]{:S(2)}, u32[]{:S(2)}) async-start(bf16[8,2,1,4,128,128]{5,4,3,1,2,0:T(8,128)(2,1)} %copy.90), calls=%async_computation.2 | async-start | bytes 4194304 | tf_op jit(solution)/shard_map/all_to_all | solution.py:30
  65.9 347.3 %all-reduce.5.cloned.1.call-start = ((), (), s32[]{:S(2)}) async-start(), calls=%async_computation.4 | async-start | bytes 8388608 | tf_op jit(solution)/shard_map/psum | solution.py:42
  106.6 371.5 %all-reduce.7.cloned.1.call-start = ((), (), s32[]{:S(2)}) async-start(), calls=%async_computation.5 | async-start | bytes 8388608 | tf_op jit(solution)/shard_map/psum | solution.py:42
  106.7 3.4 copy-start.3
  420.3 12.2 %copy-start.1 = (bf16[16,4,128,128]{3,1,2,0:T(4,128)(2,1)S(1)}, bf16[16,4,128,128]{3,1,2,0:T(4,128)(2,1)}, u32[]{:S(2)}) copy-start(bf16[16,4,128,128]{3,1,2,0:T(4,128)(2,1)} %get-tuple-element.24) | copy-start | bytes 6291460
  478.1 4.0 copy-start.2
  482.1 12.2 %slice-start = ((s8[12582912]{0:T(1024)(128)(4,1)}), s8[4194304]{0:T(1024)(128)(4,1)S(1)}, s32[]{:S(2)}) async-start(s8[12582912]{0:T(1024)(128)(4,1)} %bitcast.72), calls=%async_computation.6 | async-start | bytes 8388608
  484.4 9.9 %slice-start.1 = ((s8[12582912]{0:T(1024)(128)(4,1)}), s8[4194304]{0:T(1024)(128)(4,1)S(1)}, s32[]{:S(2)}) async-start(s8[12582912]{0:T(1024)(128)(4,1)} %bitcast.72), calls=%async_computation.7 | async-start | bytes 8388608
  484.4 9.9 %slice-start.2 = ((s8[12582912]{0:T(1024)(128)(4,1)}), s8[4194304]{0:T(1024)(128)(4,1)S(1)}, s32[]{:S(2)}) async-start(s8[12582912]{0:T(1024)(128)(4,1)} %bitcast.72), calls=%async_computation.8 | async-start | bytes 8388608
Sparse Core Ops, SparseCore 0:
  106.7 147.2 all-reduce.4
  256.6 187.8 all-reduce.6
where the time goes:
time: 569 us; the launch traced here: 568 us
  blocking collectives  334 us (59%)
  local copies, waits for them, and re-layouts  56.7 us (10%)
  matrix products  54.8 us (10%)
  waiting for transfers between devices  51.8 us (9%)
  other arithmetic  39.6 us (7%)
  between operations  17.4 us (3%)
  starting transfers between devices  13.7 us (2%)
    all_gather x1, blocking collectives, per_device(): every_columns = lax.all_gather(tile_columns, ROW_COL, axis=0, tiled=True)  301 us
    dot_general x1, matrix products, per_device(): jnp.dot(left_dense, all_panels, preferred_element_type=jnp.float32)  31.4 us
    all_to_all x1, blocking collectives, copy_for_each(): lax.all_to_all(jnp.broadcast_to(x[None], (peers, *x.shape)), axis, 0, 0,...  26.1 us
    all_to_all x1, waiting for transfers between devices, moved_by_axis(): out = lax.all_to_all(out, axes[k], k, k, tiled=True)  25.7 us
    all_to_all x1, waiting for transfers between devices, per_device(): lax.all_to_all(tile_values, 'col', split_axis=1, concat_axis=0, tiled=True)  25.3 us
    convert_element_type x2, local copies, waits for them, and re-layouts, densify(): spread.astype(jnp.bfloat16).reshape(values_in.shape[0], TILE, SLAB * TILE)  24.2 us
    concatenate x1, local copies, waits for them, and re-layouts, per_device(): jnp.concatenate(panels, axis=0)  16.6 us
    dot_general x2, matrix products, densify(): jnp.einsum('nkab,nkj->najb', values_in, picker, preferred_element_type=jn...  13.5 us
  transfers between devices with their start and end apart: 4, of which 2 were waited for; matrix products, arithmetic and copies ran while one was open for 13% of the time, Pallas kernels for 0%

commit v1 on v0

v1 whole, which is shorter than its diff:
```python
import functools

import jax
import jax.numpy as jnp
from jax import lax
from jax.experimental import pallas as pl
from jax.experimental.pallas import tpu as pltpu
from jax.sharding import PartitionSpec as P

TILE = 128
KB = 4
SLAB = 12
SECTIONS = 2
ROWS = 16
COLS = 8
BLOCK_COLS = 32
STRIP = TILE // COLS
ENTRIES = SECTIONS * KB
PANEL = SECTIONS * ROWS
FAST = (5, 64, 6)
FULL = (8, 128, 8)
MESH = pl.DeviceIdType.MESH
VMEM = pl.BlockSpec(memory_space=pltpu.VMEM)
SMEM = pl.BlockSpec(memory_space=pltpu.SMEM)
ANY = pl.BlockSpec(memory_space=pl.ANY)
BIG = 60 << 20


def params(**kw):
    return pltpu.CompilerParams(vmem_limit_bytes=BIG, **kw)


def prep_kernel(cap, owner, sections, cols, where, send_row, row_from, panel_from, picks):
    r, c = where[0], where[1]
    sec0, sec1 = sections[0], sections[1]

    def per_group(g, _):
        def per_row(j, _):
            block = owner[g * ROWS + j] // ROWS

            @pl.when(block == r)
            def _():
                row_from[g] = j

            @pl.when(block == sec0)
            def _():
                panel_from[g] = j

            @pl.when(block == sec1)
            def _():
                panel_from[ROWS + g] = j

            return 0

        return lax.fori_loop(0, ROWS, per_row, 0)

    lax.fori_loop(0, ROWS, per_group, 0)

    def per_own(j, _):
        send_row[owner[r * ROWS + j] // ROWS] = j
        return 0

    lax.fori_loop(0, ROWS, per_own, 0)
    wanted = []
    for i in range(2):
        block = owner[r * ROWS + c * 2 + i] // ROWS
        wanted.append((block == sec0) | (block == sec1))

    def per_block(b, _):
        for m in range(cap):
            picks[b * cap + m] = 0
        count = jnp.int32(0)
        for i in range(2):
            for k in range(KB):
                rel = cols[i * BLOCK_COLS + b * KB + k] - b * BLOCK_COLS
                take = wanted[i] & (rel >= 0) & (rel < SLAB)

                @pl.when(take & (count < cap))
                def _():
                    picks[b * cap + count] = i * KB + k

                count = count + take.astype(jnp.int32)
        return 0

    lax.fori_loop(0, COLS, per_block, 0)


def prep(cap, owner, sections, cols, where):
    i32 = jnp.int32
    return pl.pallas_call(
        functools.partial(prep_kernel, cap),
        out_shape=(
            jax.ShapeDtypeStruct((ROWS,), i32),
            jax.ShapeDtypeStruct((ROWS,), i32),
            jax.ShapeDtypeStruct((2 * ROWS,), i32),
            jax.ShapeDtypeStruct((COLS * cap,), i32),
        ),
        in_specs=[SMEM] * 4,
        out_specs=(SMEM,) * 4,
    )(owner, sections, cols, where)


def spread_kernel(
    cap, tv, idx, sections, send_row, picks,
    strips, cand, lists,
    left_out, left_in, right_out, row_out,
    s_idx, r_idx, s_left, r_left, s_right, r_right, s_list, r_list, s_row, r_row,
):
    r, c = lax.axis_index("row"), lax.axis_index("col")
    barrier = pltpu.get_barrier_semaphore()
    for d in range(1, COLS):
        pl.semaphore_signal(barrier, inc=1, device_id={"col": (c + d) % COLS}, device_id_type=MESH)
    for d in range(1, ROWS):
        pl.semaphore_signal(barrier, inc=1, device_id={"row": (r + d) % ROWS}, device_id_type=MESH)
    for i in range(2):
        for s in range(SECTIONS):
            source = sections[s] // 2
            for k in range(KB):
                for h in range(COLS):
                    left_out[h, i * ENTRIES + s * KB + k] = tv[
                        i, source * KB + k, h * STRIP : (h + 1) * STRIP, :
                    ]

    def pack(b, _):
        for m in range(cap):
            e = picks[b * cap + m]
            right_out[b, m] = tv[e // KB, b * KB + e % KB]
        return 0

    lax.fori_loop(0, COLS, pack, 0)
    lists[r, c] = idx[...]
    left_in[c] = left_out[c]
    cand[c] = right_out[c]
    pl.semaphore_wait(barrier, COLS - 1 + ROWS - 1)

    idx_copies, left_copies, right_copies = [], [], []
    for d in range(1, COLS):
        to = (c + d) % COLS
        copy = pltpu.make_async_remote_copy(
            idx, lists.at[r, c], s_idx.at[d], r_idx.at[d], device_id={"col": to}, device_id_type=MESH
        )
        copy.start()
        idx_copies.append(copy)
    for d in range(1, COLS):
        to = (c + d) % COLS
        copy = pltpu.make_async_remote_copy(
            left_out.at[to], left_in.at[c], s_left.at[d], r_left.at[d],
            device_id={"col": to}, device_id_type=MESH,
        )
        copy.start()
        left_copies.append(copy)
    for d in range(1, COLS):
        to = (c + d) % COLS
        copy = pltpu.make_async_remote_copy(
            right_out.at[to], cand.at[c], s_right.at[d], r_right.at[d],
            device_id={"col": to}, device_id_type=MESH,
        )
        copy.start()
        right_copies.append(copy)
    for copy in idx_copies:
        copy.wait_recv()
    list_copies = []
    for d in range(1, ROWS):
        to = (r + d) % ROWS
        copy = pltpu.make_async_remote_copy(
            lists.at[r], lists.at[r], s_list.at[d], r_list.at[d],
            device_id={"row": to}, device_id_type=MESH,
        )
        copy.start()
        list_copies.append(copy)
    for copy in left_copies:
        copy.wait_recv()

    def reorder(t, _):
        j = send_row[t]
        for e in range(ENTRIES):
            row_out[t, e] = left_in[j // 2, (j % 2) * ENTRIES + e]
        return 0

    lax.fori_loop(0, ROWS, reorder, 0)
    strips[r] = row_out[r]
    row_copies = []
    for d in range(1, ROWS):
        to = (r + d) % ROWS
        copy = pltpu.make_async_remote_copy(
            row_out.at[to], strips.at[r], s_row.at[d], r_row.at[d],
            device_id={"row": to}, device_id_type=MESH,
        )
        copy.start()
        row_copies.append(copy)
    for copy in list_copies + row_copies + right_copies:
        copy.wait_recv()
    for copy in idx_copies + left_copies + right_copies + list_copies + row_copies:
        copy.wait_send()


def spread(cap, collective_id, tv, idx, sections, send_row, picks):
    bf = jnp.bfloat16
    dma = pltpu.SemaphoreType.DMA
    return pl.pallas_call(
        functools.partial(spread_kernel, cap),
        out_shape=(
            jax.ShapeDtypeStruct((ROWS, ENTRIES, STRIP, TILE), bf),
            jax.ShapeDtypeStruct((COLS, cap, TILE, TILE), bf),
            jax.ShapeDtypeStruct((ROWS, COLS, 1, TILE), jnp.int32),
        ),
        in_specs=[VMEM, VMEM, SMEM, SMEM, SMEM],
        out_specs=(VMEM, VMEM, VMEM),
        scratch_shapes=[
            pltpu.VMEM((COLS, 2 * ENTRIES, STRIP, TILE), bf),
            pltpu.VMEM((COLS, 2 * ENTRIES, STRIP, TILE), bf),
            pltpu.VMEM((COLS, cap, TILE, TILE), bf),
            pltpu.VMEM((ROWS, ENTRIES, STRIP, TILE), bf),
        ]
        + [dma((COLS,))] * 6
        + [dma((ROWS,))] * 4,
        compiler_params=params(collective_id=collective_id, has_side_effects=True),
    )(tv, idx, sections, send_row, picks)


def lists_kernel(
    caps, lists, owner, sections, where, row_from, panel_from,
    keep_left, row_left, inner_left, keep_right, start, count, col_right, totals,
):
    cap, cap_left, cap_group = caps
    r, c = where[0], where[1]
    for m in range(cap_group):
        keep_right[m] = 0

    def clear(m, _):
        keep_left[m] = 0
        return 0

    lax.fori_loop(0, cap_left, clear, 0)

    def left(g, n):
        j = row_from[g]
        line = g * COLS + j // 2
        base = (j % 2) * BLOCK_COLS
        p = owner[g * ROWS + j] - r * ROWS
        for s in range(SECTIONS):
            sec = sections[s]
            for k in range(KB):
                rel = lists[line, base + (sec // 2) * KB + k] - sec * ROWS
                take = (rel >= 0) & (rel < ROWS)

                @pl.when(take)
                def _():
                    keep_left[n] = g * ENTRIES + s * KB + k
                    row_left[n] = p
                    inner_left[n] = s * ROWS + rel

                n = n + take.astype(jnp.int32)
        return n

    totals[0] = lax.fori_loop(0, ROWS, left, jnp.int32(0))

    def right(g, _):
        a, b = panel_from[g], panel_from[ROWS + g]
        swap = b < a
        n = jnp.int32(0)
        used = jnp.int32(0)
        for order in range(2):
            s = (swap if order == 0 else jnp.logical_not(swap)).astype(jnp.int32)
            j = jnp.where(s == 0, a, b)
            other = jnp.where(s == 0, b, a)
            if order == 1:
                used = jnp.where(j // 2 == other // 2, used, 0)
            sec = sections[s]
            q = s * ROWS + owner[g * ROWS + j] - sec * ROWS
            line = g * COLS + j // 2
            base = (j % 2) * BLOCK_COLS + c * KB
            start[q] = g * cap_group + n
            first = n
            for k in range(KB):
                rel = lists[line, base + k] - c * BLOCK_COLS
                take = (rel >= 0) & (rel < SLAB)

                @pl.when(take)
                def _():
                    col_right[g * cap_group + n] = rel

                @pl.when(take & (g == r))
                def _():
                    keep_right[n] = (j // 2) * cap + used

                n = n + take.astype(jnp.int32)
                used = used + take.astype(jnp.int32)
            count[q] = n - first
        return 0

    lax.fori_loop(0, ROWS, right, 0)


def make_lists(caps, lists, owner, sections, where, row_from, panel_from):
    cap, cap_left, cap_group = caps
    sizes = (cap_left, cap_left, cap_left, cap_group, PANEL, PANEL, ROWS * cap_group, 1)
    return pl.pallas_call(
        functools.partial(lists_kernel, caps),
        out_shape=tuple(jax.ShapeDtypeStruct((n,), jnp.int32) for n in sizes),
        in_specs=[SMEM] * 6,
        out_specs=(SMEM,) * len(sizes),
    )(lists, owner, sections, where, row_from, panel_from)


def gather_kernel(caps, strips, cand, keep_left, keep_right, left, right, send, recv):
    cap, cap_left, cap_group = caps
    r, c = lax.axis_index("row"), lax.axis_index("col")
    cut = cap_left * 9 // 16
    a_part, b_part = (0, cut), (cut, cap_left)
    halves = lambda part: ((part[0], (part[0] + part[1]) // 2), ((part[0] + part[1]) // 2, part[1]))
    g_part = (0, cap_group)
    zp = {"col": c + 1 - 2 * (c % 2)}
    yn, yb = {"col": (c + 2) % COLS}, {"col": (c + COLS - 2) % COLS}
    core = {"row": r + 1 - 2 * (r % 2)}
    zh = {"row": (r // 4) * 4 + (r + 2) % 4}
    xn, xb = {"row": (r + 4) % ROWS}, {"row": (r + ROWS - 4) % ROWS}
    barrier = pltpu.get_barrier_semaphore()
    for peer in (zp, yn, yb, core, zh, xn, xb):
        pl.semaphore_signal(barrier, inc=1, device_id=peer, device_id_type=MESH)

    def pack_left(m, _):
        e = keep_left[m]
        left[c, m] = strips[e // ENTRIES, e % ENTRIES]
        return 0

    lax.fori_loop(0, cap_left, pack_left, 0)

    def pack_right(m, _):
        e = keep_right[m]
        right[r, m] = cand[e // cap, e % cap]
        return 0

    lax.fori_loop(0, cap_group, pack_right, 0)
    pl.semaphore_wait(barrier, 7)

    started = []

    def go(buf, origin, part, to):
        n = len(started)
        piece = buf.at[origin, pl.ds(part[0], part[1] - part[0])]
        copy = pltpu.make_async_remote_copy(
            piece, piece, send.at[n], recv.at[n], device_id=to, device_id_type=MESH
        )
        copy.start()
        started.append(copy)
        return copy

    cz = c + 1 - 2 * (c % 2)
    c_m, c_p, c_o = (c + COLS - 2) % COLS, (c + 2) % COLS, (c + 4) % COLS
    z_m, z_p, z_o = (cz + COLS - 2) % COLS, (cz + 2) % COLS, (cz + 4) % COLS
    rz = (r // 4) * 4 + (r + 2) % 4
    r_m, r_p, r_o = (r + ROWS - 4) % ROWS, (r + 4) % ROWS, (r + 8) % ROWS
    q_m, q_p, q_o = (rz + ROWS - 4) % ROWS, (rz + 4) % ROWS, (rz + 8) % ROWS
    a1, a2 = halves(a_part)
    b1, b2 = halves(b_part)
    g1, g2 = halves(g_part)

    k1 = go(left, c, a_part, zp)
    k21 = go(right, r, g_part, zh)
    k10 = go(left, c, b_part, yn)
    k11 = go(left, c, b_part, yb)
    k22 = go(right, r, g_part, xn)
    k23 = go(right, r, g_part, xb)
    k2 = go(left, c, a_part, yn)
    k3 = go(left, c, a_part, yb)
    k12 = go(left, c, b_part, zp)
    k20 = go(right, r, g_part, core)
    done = []

    def arrived(copy):
        copy.wait_recv()
        done.append(copy)

    arrived(k10)
    k13 = go(left, c_m, b1, yn)
    k14 = go(left, c_m, b_part, zp)
    arrived(k11)
    k15 = go(left, c_p, b2, yb)
    k16 = go(left, c_p, b_part, zp)
    arrived(k1)
    k4 = go(left, cz, a_part, yn)
    k5 = go(left, cz, a_part, yb)
    arrived(k21)
    k24 = go(right, rz, g_part, xn)
    k25 = go(right, rz, g_part, xb)
    k26 = go(right, rz, g_part, core)
    arrived(k22)
    k27 = go(right, r_m, g1, xn)
    k28 = go(right, r_m, g_part, core)
    arrived(k23)
    k29 = go(right, r_p, g2, xb)
    k30 = go(right, r_p, g_part, core)
    arrived(k2)
    k6 = go(left, c_m, a1, yn)
    arrived(k3)
    k7 = go(left, c_p, a2, yb)
    arrived(k13)
    k17 = go(left, c_o, b1, zp)
    arrived(k15)
    k18 = go(left, c_o, b2, zp)
    arrived(k24)
    k31 = go(right, q_m, g1, xn)
    k32 = go(right, q_m, g_part, core)
    arrived(k25)
    k33 = go(right, q_p, g2, xb)
    k34 = go(right, q_p, g_part, core)
    arrived(k4)
    k8 = go(left, z_m, a1, yn)
    arrived(k5)
    k9 = go(left, z_p, a2, yb)
    arrived(k27)
    k35 = go(right, r_o, g1, core)
    arrived(k29)
    k36 = go(right, r_o, g2, core)
    arrived(k31)
    k37 = go(right, q_o, g1, core)
    arrived(k33)
    k38 = go(right, q_o, g2, core)
    for copy in started:
        if not any(copy is other for other in done):
            copy.wait_recv()
    for copy in started:
        copy.wait_send()


COPIES = 37


def gather(caps, collective_id, strips, cand, keep_left, keep_right):
    cap, cap_left, cap_group = caps
    bf = jnp.bfloat16
    return pl.pallas_call(
        functools.partial(gather_kernel, caps),
        out_shape=(
            jax.ShapeDtypeStruct((COLS, cap_left, STRIP, TILE), bf),
            jax.ShapeDtypeStruct((ROWS, cap_group, TILE, TILE), bf),
        ),
        in_specs=[VMEM, VMEM, SMEM, SMEM],
        out_specs=(VMEM, VMEM),
        scratch_shapes=[pltpu.SemaphoreType.DMA((COPIES,))] * 2,
        compiler_params=params(collective_id=collective_id, has_side_effects=True),
    )(strips, cand, keep_left, keep_right)


OUT_TILES = ROWS * SLAB
UNROLL = 4


def product_kernel(
    caps, left, right, row_left, inner_left, start, count, col_right, totals,
    squares, slot_of, sums,
    acc, job_left, job_right, job_slot, job_first, out_of, part, sem,
):
    cap, cap_left, cap_group = caps

    def clear(o, _):
        slot_of[o] = -1
        return 0

    lax.fori_loop(0, OUT_TILES, clear, 0)

    def per_left(m, carry):
        p, q = row_left[m], inner_left[m]
        base = start[q]

        def per_right(t, carry):
            n, touched = carry
            o = p * SLAB + col_right[base + t]
            old = slot_of[o]
            fresh = old < 0
            slot = jnp.where(fresh, touched, old)
            job_left[n] = m
            job_right[n] = base + t
            job_slot[n] = slot
            job_first[n] = fresh.astype(jnp.int32)
            slot_of[o] = slot
            out_of[slot] = o
            return n + 1, touched + fresh.astype(jnp.int32)

        return lax.fori_loop(0, count[q], per_right, carry)

    n, touched = lax.fori_loop(0, totals[0], per_left, (jnp.int32(0), jnp.int32(0)))
    for u in range(UNROLL):
        job_left[n + u] = 0
        job_right[n + u] = 0
        job_slot[n + u] = OUT_TILES
        job_first[n + u] = 1

    def multiply(g, _):
        results = []
        for u in range(UNROLL):
            a = left[:, job_left[g * UNROLL + u]].reshape(TILE, TILE)
            e = job_right[g * UNROLL + u]
            b = right[e // cap_group, e % cap_group]
            results.append(jnp.dot(a, b, preferred_element_type=jnp.float32))
        for u in range(UNROLL):
            slot = job_slot[g * UNROLL + u]
            keep = (1 - job_first[g * UNROLL + u]).astype(jnp.float32)
            old = acc[slot]
            acc[slot] = results[u] + jnp.where(keep > 0, old, 0.0)
        return 0

    lax.fori_loop(0, (n + UNROLL - 1) // UNROLL, multiply, 0)
    part[...] = jnp.zeros_like(part)

    def finish(slot, _):
        value = acc[slot]
        value = value * value
        acc[slot] = value
        pltpu.make_async_copy(acc.at[slot], squares.at[slot], sem).start()
        col = out_of[slot] % SLAB
        part[col] += value.reshape(TILE // 8, 8, TILE).sum(axis=0)
        return 0

    lax.fori_loop(0, touched, finish, 0)
    sums[...] = part[...].sum(axis=1)

    def drain(slot, _):
        pltpu.make_async_copy(acc.at[slot], squares.at[slot], sem).wait()
        return 0

    lax.fori_loop(0, touched, drain, 0)


def products(caps, left, right, row_left, inner_left, start, count, col_right, totals):
    cap, cap_left, cap_group = caps
    jobs = cap_left * KB + UNROLL
    f32, i32 = jnp.float32, jnp.int32
    return pl.pallas_call(
        functools.partial(product_kernel, caps),
        out_shape=(
            jax.ShapeDtypeStruct((OUT_TILES, TILE, TILE), f32),
            jax.ShapeDtypeStruct((OUT_TILES,), i32),
            jax.ShapeDtypeStruct((ROWS, TILE), f32),
        ),
        in_specs=[VMEM, VMEM] + [SMEM] * 6,
        out_specs=(ANY, SMEM, VMEM),
        scratch_shapes=[pltpu.VMEM((OUT_TILES + 1, TILE, TILE), f32)]
        + [pltpu.SMEM((jobs,), i32)] * 4
        + [pltpu.SMEM((OUT_TILES,), i32), pltpu.VMEM((ROWS, 8, TILE), f32), pltpu.SemaphoreType.DMA],
        compiler_params=params(),
    )(left, right, row_left, inner_left, start, count, col_right, totals)


def total_kernel(mine, out, parts, send, recv):
    r = lax.axis_index("row")
    barrier = pltpu.get_barrier_semaphore()
    for d in range(1, ROWS):
        pl.semaphore_signal(barrier, inc=1, device_id={"row": (r + d) % ROWS}, device_id_type=MESH)
    parts[r] = mine[...]
    pl.semaphore_wait(barrier, ROWS - 1)
    copies = []
    for d in range(1, ROWS):
        copy = pltpu.make_async_remote_copy(
            mine, parts.at[r], send.at[d], recv.at[d],
            device_id={"row": (r + d) % ROWS}, device_id_type=MESH,
        )
        copy.start()
        copies.append(copy)
    for copy in copies:
        copy.wait_recv()
    out[...] = parts[...].sum(axis=0)
    for copy in copies:
        copy.wait_send()


def total(collective_id, mine):
    return pl.pallas_call(
        total_kernel,
        out_shape=jax.ShapeDtypeStruct((ROWS, TILE), jnp.float32),
        in_specs=[VMEM],
        out_specs=VMEM,
        scratch_shapes=[
            pltpu.VMEM((ROWS, ROWS, TILE), jnp.float32),
            pltpu.SemaphoreType.DMA((ROWS,)),
            pltpu.SemaphoreType.DMA((ROWS,)),
        ],
        compiler_params=params(collective_id=collective_id, has_side_effects=True),
    )(mine)


def write_kernel(squares, slot_of, totals, out, tiles, block, factor, in_sem, out_sem):
    count = float(ROWS * ROWS * TILE)
    factor[...] = count / (totals[...] + 1e-06)

    def fetch(o, _):
        slot = slot_of[o]

        @pl.when(slot >= 0)
        def _():
            pltpu.make_async_copy(squares.at[slot], tiles.at[o], in_sem).start()

        return 0

    lax.fori_loop(0, OUT_TILES, fetch, 0)

    def got(o, _):
        @pl.when(slot_of[o] >= 0)
        def _():
            pltpu.make_async_copy(squares.at[0], tiles.at[o], in_sem).wait()

        return 0

    lax.fori_loop(0, OUT_TILES, got, 0)

    def per_row(p, _):
        for col in range(SLAB):
            slot = slot_of[p * SLAB + col]

            @pl.when(slot >= 0)
            def _():
                value = tiles[p * SLAB + col] * factor[col : col + 1, :]
                block[p, :, col * TILE : (col + 1) * TILE] = value.astype(jnp.bfloat16)

            @pl.when(slot < 0)
            def _():
                block[p, :, col * TILE : (col + 1) * TILE] = jnp.zeros((TILE, TILE), jnp.bfloat16)

        pltpu.make_async_copy(block.at[p], out.at[pl.ds(p * TILE, TILE)], out_sem).start()
        return 0

    lax.fori_loop(0, ROWS, per_row, 0)

    def drain(p, _):
        pltpu.make_async_copy(block.at[p], out.at[pl.ds(p * TILE, TILE)], out_sem).wait()
        return 0

    lax.fori_loop(0, ROWS, drain, 0)


def write(squares, slot_of, totals):
    return pl.pallas_call(
        write_kernel,
        out_shape=jax.ShapeDtypeStruct((ROWS * TILE, SLAB * TILE), jnp.bfloat16),
        in_specs=[ANY, SMEM, VMEM],
        out_specs=ANY,
        scratch_shapes=[
            pltpu.VMEM((OUT_TILES, TILE, TILE), jnp.float32),
            pltpu.VMEM((ROWS, TILE, SLAB * TILE), jnp.bfloat16),
            pltpu.VMEM((ROWS, TILE), jnp.float32),
            pltpu.SemaphoreType.DMA,
            pltpu.SemaphoreType.DMA,
        ],
        compiler_params=params(),
    )(squares, slot_of, totals)


def overflow(lists, owner, sections):
    tiles = owner.shape[0]
    cols = lists[:, :, 0, : 2 * BLOCK_COLS].reshape(tiles, COLS, KB)
    block = owner // ROWS
    panel = (block == sections[0]) | (block == sections[1])
    rel = cols - (jnp.arange(COLS, dtype=jnp.int32) * BLOCK_COLS)[None, :, None]
    slab = ((rel >= 0) & (rel < SLAB) & panel[:, None, None]).astype(jnp.int32).sum(axis=2)
    pairs = slab.reshape(tiles // 2, 2, COLS).sum(axis=1)
    groups = slab.reshape(ROWS, ROWS, COLS).sum(axis=1)
    inner = jnp.zeros((tiles,), jnp.int32)
    for s in range(SECTIONS):
        off = cols - sections[s] * ROWS
        inner = inner + ((off >= 0) & (off < ROWS)).astype(jnp.int32).sum(axis=(1, 2))
    mine = (block[:, None] == jnp.arange(ROWS, dtype=jnp.int32)[None, :]).astype(jnp.int32)
    rows = (mine * inner[:, None]).sum(axis=0)
    return (pairs.max() > FAST[0]) | (rows.max() > FAST[1]) | (groups.max() > FAST[2])


def per_device(tile_values, tile_columns, owner_map, section_rows):
    where = jnp.stack([lax.axis_index("row"), lax.axis_index("col")]).astype(jnp.int32)
    flat = tile_columns.reshape(-1)
    idx = jnp.pad(flat, (0, TILE - flat.shape[0])).reshape(1, TILE)
    tv = tile_values.reshape(2, COLS * KB, TILE, TILE)

    def first(caps, collective_id):
        send_row, row_from, panel_from, picks = prep(caps[0], owner_map, section_rows, flat, where)
        strips, cand, lists = spread(caps[0], collective_id, tv, idx, section_rows, send_row, picks)
        return strips, cand, lists, row_from, panel_from

    def rest(caps, ids, strips, cand, lists, row_from, panel_from):
        made = make_lists(
            caps, lists.reshape(ROWS * COLS, TILE), owner_map, section_rows, where, row_from, panel_from
        )
        keep_left, row_left, inner_left, keep_right, start, count, col_right, totals = made
        left, right = gather(caps, ids[0], strips, cand, keep_left, keep_right)
        squares, slot_of, sums = products(
            caps, left, right, row_left, inner_left, start, count, col_right, totals
        )
        return write(squares, slot_of, total(ids[1], sums))

    got = first(FAST, 0)
    flag = overflow(got[2], owner_map, section_rows)
    return lax.cond(
        flag,
        lambda *_: rest(FULL, (4, 5), *first(FULL, 3)),
        lambda *args: rest(FAST, (1, 2), *args),
        *got,
    )


def solution(mesh):
    both = ("row", "col")
    in_specs = (P(both, None, None, None, None), P(both, None, None), P(), P())
    return jax.shard_map(
        per_device, mesh=mesh, in_specs=in_specs, out_specs=P("row", "col"), check_vma=False
    )
```

time: 569 us -> 125 us (0.22)
  blocking collectives: 334 us -> 0 us
  Pallas kernels: 0 us -> 114 us
  matrix products: 54.8 us -> 0 us
  local copies, waits for them, and re-layouts: 56.7 us -> 3.58 us
  waiting for transfers between devices: 51.8 us -> 0 us
  other arithmetic: 39.6 us -> 4.43 us
  between operations: 17.4 us -> 3.42 us
  starting transfers between devices: 13.7 us -> 0 us
    all_gather x1 -> x0, blocking collectives: 301 us -> none  [per_device(): every_columns = lax.all_gather(tile_columns, ROW_COL, axis=0, tiled=True)]
    pallas_call x0 -> x7, Pallas kernels: none -> 114 us  [the longest x1 42.3 us: spread(): pl.pallas_call(functools.partial(spread_kernel, cap), out_shape=(jax.Shap...]
    dot_general x4 -> x0, matrix products: 54.8 us -> none  [the longest x1 31.4 us: per_device(): jnp.dot(left_dense, all_panels, preferred_element_type=jnp.float32)]
    all_to_all x2 -> x0, waiting for transfers between devices: 51.1 us -> none  [the longest x1 25.7 us: moved_by_axis(): out = lax.all_to_all(out, axes[k], k, k, tiled=True)]
    all_to_all x2 -> x0, blocking collectives: 32.7 us -> none  [the longest x1 26.1 us: copy_for_each(): lax.all_to_all(jnp.broadcast_to(x[None], (peers, *x.shape)), axis, 0, 0,...]
    convert_element_type x4 -> x0, local copies, waits for them, and re-layouts: 24.4 us -> none  [the longest x2 24.2 us: densify(): spread.astype(jnp.bfloat16).reshape(values_in.shape[0], TILE, SLAB * TILE)]
    concatenate x2 -> x0, local copies, waits for them, and re-layouts: 16.7 us -> none  [the longest x1 16.6 us: per_device(): jnp.concatenate(panels, axis=0)]
    all_to_all x2 -> x0, starting transfers between devices: 13.7 us -> none  [the longest x1 7.17 us: moved_by_axis(): out = lax.all_to_all(out, axes[k], k, k, tiled=True)]
  transfers between devices with their start and end apart: 4 -> 0, of which waited for: 2 -> 0; matrix products, arithmetic and copies ran while one was open for 13% -> 0% of each run, Pallas kernels for 0% -> 0%
where the time goes in v1:
time: 125 us
  Pallas kernels  114 us (91%)
  other arithmetic  4.43 us (4%)
  local copies, waits for them, and re-layouts  3.58 us (3%)
  between operations  3.42 us (3%)
    pallas_call x1, Pallas kernels, spread(): pl.pallas_call(functools.partial(spread_kernel, cap), out_shape=(jax.Shap...  42.3 us
    pallas_call x1, Pallas kernels, gather(): pl.pallas_call(functools.partial(gather_kernel, caps), out_shape=(jax.Sha...  31.8 us
    pallas_call x1, Pallas kernels, products(): pl.pallas_call(functools.partial(product_kernel, caps), out_shape=(jax.Sh...  10.6 us
    pallas_call x1, Pallas kernels, total(): pl.pallas_call(total_kernel, out_shape=jax.ShapeDtypeStruct((ROWS, TILE),...  9.46 us
    pallas_call x1, Pallas kernels, write(): pl.pallas_call(write_kernel, out_shape=jax.ShapeDtypeStruct((ROWS * TILE,...  7.9 us
    pallas_call x1, Pallas kernels, prep(): pl.pallas_call(functools.partial(prep_kernel, cap), out_shape=(jax.ShapeD...  6.51 us
    pallas_call x1, Pallas kernels, make_lists(): pl.pallas_call(functools.partial(lists_kernel, caps), out_shape=tuple((ja...  5.08 us

profile of v1, /device:TPU:1, one launch (start us, length us, event | category | flops | bytes accessed | tf_op | source)
XLA Modules:
  0.0 125.2 jit_solution(8357649305988666115)
XLA Ops:
  0.0 0.1 pad_add_fusion.where
  0.1 1.5 %fusion = (s32[1]{0:T(128)}, s32[1]{0:T(128)}) fusion(s32[2]{0:T(128)} %sections.3), kind=kLoop, calls=%fused_computation.15 | loop fusion | bytes 16 | tf_op jit(solution)/shard_map/slice | solution.py:653
  2.9 2.0 %compare_or_fusion = (pred[256]{0:T(512)(128)(4,1)S(1)}, s32[256]{0:T(256)S(1)}) fusion(s32[]{:T(128)} %bitcast.9, s32[]{:T(128)} %bitcast.8, s32[256]{0:T(256)} %owner.1), kind=kLoop, calls=%fused_computation.7 | loop fusion | flops 4608 | bytes 2312 | tf_op jit(solution)/shard_map/or | solution.py:653
  4.9 0.8 copy.26
  5.7 0.1 reshape.33.cols
  5.8 6.5 %shard_map.48 = (s32[16]{0:T(128)}, s32[16]{0:T(128)S(1)}, s32[32]{0:T(128)S(1)}, s32[40]{0:T(128)}) custom-call(s32[256]{0:T(256)} %owner.1, s32[2]{0:T(128)} %sections.3, s32[64]{0:T(128)S(1)} %reshape.33.cols, s32[2]{0:T(128)S(1)} %pad_add_fusion.where), custom_call_target="tpu_custom_call" | custom-call | tf_op jit(solution)/shard_map/pallas_call | solution.py:90
  12.3 42.3 %shard_map.49 = (bf16[16,8,16,128]{3,2,1,0:T(8,128)(2,1)}, bf16[8,5,128,128]{3,2,1,0:T(8,128)(2,1)}, s32[16,8,1,128]{3,2,1,0:T(1,128)S(1)}) custom-call(bf16[2,32,128,128]{3,2,1,0:T(8,128)(2,1)} %bitcast.14, s32[1,128]{1,0:T(1,128)S(1)} %pad_bitcast_fusion.idx, s32[2]{0:T(128)} %sections.3, s32[16]{0:T(128)} %get-tuple-element.90.send_row, ...), custom_call_target="tpu_custom_call" | custom-call | tf_op jit(solution)/shard_map/pallas_call | solution.py:200
  54.7 0.2 slice_reduce_fusion
  54.9 0.6 reshape_squeeze.3
  55.4 0.4 copy.27
  55.8 0.1 convert_reduce_fusion
  55.9 0.1 select_reduce_fusion
  56.0 0.6 reduce_max.28
  57.3 0.1 copy.38
  57.5 0.6 reduce_max.29
  58.8 0.2 reduce_sum.55
  59.0 0.6 reduce_max.27
  60.3 0.0 copy-done.1
  60.3 64.9 %conditional.1 = (bf16[2048,1536]{1,0:T(8,128)(2,1)}) conditional(s32[]{:T(128)} %convert_element_type.16, (s32[16,8,1,128]{3,2,1,0:T(1,128)S(1)}, s32[256]{0:T(256)S(1)}, s32[2]{0:T(128)S(1)}, s32[2]{0:T(128)S(1)}, s32[16]{0:T(128)S(1)}, /*index=5*/s32[32]{0:T(128)S(1)}, bf16[16,8,16,128]{3,2,1,0:T(8,128)(2,1)}, ...), branch_computations={%region_9.10_spmd, %region_10.11_spmd} | conditional | bytes 8 | solution.py:691
  60.3 5.1 %branch_0_fun.5 = (s32[64]{0:T(128)}, s32[64]{0:T(128)}, s32[64]{0:T(128)}, s32[6]{0:T(128)}, s32[32]{0:T(128)}, /*index=5*/s32[32]{0:T(128)}, s32[96]{0:T(128)}, s32[1]{0:T(128)}) custom-call(s32[128,128]{1,0:T(8,128)S(1)} %bitcast.17, s32[256]{0:T(256)S(1)} %get-tuple-element.39.owner, s32[2]{0:T(128)S(1)} %get-tuple-element.40.sections, ...), custom_call_target="tpu_custom_call" | custom-call | tf_op jit(solution)/shard_map/cond/branch_0_fun/pallas_call | solution.py:298
  65.4 31.8 %branch_0_fun.6 = (bf16[8,64,16,128]{3,2,1,0:T(8,128)(2,1)}, bf16[16,6,128,128]{3,2,1,0:T(8,128)(2,1)}) custom-call(bf16[16,8,16,128]{3,2,1,0:T(8,128)(2,1)} %get-tuple-element.36.strips, bf16[8,5,128,128]{3,2,1,0:T(8,128)(2,1)} %get-tuple-element.37.cand, s32[64]{0:T(128)} %get-tuple-element.44.keep_left, s32[6]{0:T(128)} %get-tuple-element.45.keep_right), custom_call_target="tpu_custom_call" | custom-call | tf_op jit(solution)/shard_map/cond/branch_0_fun/pallas_call | solution.py:433
  97.2 10.6 %branch_0_fun.7 = (f32[192,128,128]{2,1,0:T(8,128)}, s32[192]{0:T(256)}, f32[16,128]{1,0:T(8,128)}) custom-call(bf16[8,64,16,128]{3,2,1,0:T(8,128)(2,1)} %get-tuple-element.46.left, bf16[16,6,128,128]{3,2,1,0:T(8,128)(2,1)} %get-tuple-element.47.right, s32[64]{0:T(128)} %get-tuple-element.48.row_left, s32[64]{0:T(128)} %get-tuple-element.49.inner_left, ...), custom_call_target="tpu_custom_call" | custom-call | tf_op jit(solution)/shard_map/cond/branch_0_fun/pallas_call | solution.py:530
  107.8 9.5 %branch_0_fun.8.totals = f32[16,128]{1,0:T(8,128)} custom-call(f32[16,128]{1,0:T(8,128)} %get-tuple-element.56.mine), custom_call_target="tpu_custom_call" | custom-call | tf_op jit(solution)/shard_map/cond/branch_0_fun/pallas_call | solution.py:569
  117.3 7.9 %branch_0_fun.9 = bf16[2048,1536]{1,0:T(8,128)(2,1)} custom-call(f32[192,128,128]{2,1,0:T(8,128)} %get-tuple-element.54.squares, s32[192]{0:T(256)} %get-tuple-element.55.slot_of, f32[16,128]{1,0:T(8,128)} %branch_0_fun.8.totals), custom_call_target="tpu_custom_call" | custom-call | tf_op jit(solution)/shard_map/cond/branch_0_fun/pallas_call | solution.py:633
  (9 shorter events, 0.0 us)
Async XLA Ops:
  0.0 60.3 %copy-start.1 = (s32[2]{0:T(128)S(1)}, s32[2]{0:T(128)}, u32[]{:S(2)}) copy-start(s32[2]{0:T(128)} %sections.3) | copy-start | bytes 28
  0.0 60.3 %copy-start.2 = (s32[256]{0:T(256)S(1)}, s32[256]{0:T(256)}, u32[]{:S(2)}) copy-start(s32[256]{0:T(256)} %owner.1) | copy-start | bytes 3076
  0.0 60.3 %copy-start = (bf16[2,8,4,128,128]{4,3,2,1,0:T(8,128)(2,1)S(1)}, bf16[2,8,4,128,128]{4,3,2,1,0:T(8,128)(2,1)}, u32[]{:S(2)}) copy-start(bf16[2,8,4,128,128]{4,3,2,1,0:T(8,128)(2,1)} %param.6) | copy-start | bytes 6291460

commit v2 on v1

v2 whole, which is shorter than its diff:
```python
import functools

import jax
import jax.numpy as jnp
from jax import lax
from jax.experimental import pallas as pl
from jax.experimental.pallas import tpu as pltpu
from jax.sharding import PartitionSpec as P

TILE = 128
KB = 4
SLAB = 12
SECTIONS = 2
ROWS = 16
COLS = 8
BLOCK_COLS = 32
STRIP = TILE // COLS
ENTRIES = SECTIONS * KB
PANEL = SECTIONS * ROWS
FAST = (8, 56, 10, 16)
FULL = (16, 128, 16, 32)
MESH = pl.DeviceIdType.MESH
VMEM = pl.BlockSpec(memory_space=pltpu.VMEM)
SMEM = pl.BlockSpec(memory_space=pltpu.SMEM)
ANY = pl.BlockSpec(memory_space=pl.ANY)


def params(mib, **kw):
    return pltpu.CompilerParams(vmem_limit_bytes=mib << 20, **kw)


def prep_kernel(cap, owner, sections, cols, send_row, row_from, panel_from, picks, inverse):
    r, c = lax.axis_index("row"), lax.axis_index("col")

    def invert(g, _):
        for j in range(ROWS):
            inverse[owner[g * ROWS + j]] = g * ROWS + j
        return 0

    lax.fori_loop(0, ROWS, invert, 0)
    secs = [sections[0], sections[1]]
    for j in range(ROWS):
        send_row[owner[r * ROWS + j] >> 4] = j
        t = inverse[r * ROWS + j]
        row_from[t >> 4] = t & 15
        for s in range(SECTIONS):
            t = inverse[secs[s] * ROWS + j]
            panel_from[s * ROWS + (t >> 4)] = t & 15
    wanted = []
    for i in range(2):
        block = owner[r * ROWS + c * 2 + i] >> 4
        wanted.append((block == secs[0]) | (block == secs[1]))
    room = cap + 1

    def per_y(yd, _):
        for m in range(room):
            picks[yd * room + m] = 0
        count = jnp.int32(0)
        for i in range(2):
            for z in range(2):
                b = yd * 2 + z
                for k in range(KB):
                    rel = cols[i * BLOCK_COLS + b * KB + k] - b * BLOCK_COLS
                    take = wanted[i] & (rel >= 0) & (rel < SLAB)
                    picks[yd * room + count] = i * BLOCK_COLS + b * KB + k
                    count = jnp.minimum(count + take.astype(jnp.int32), cap)
        return 0

    lax.fori_loop(0, 4, per_y, 0)


def prep(cap, owner, sections, cols):
    i32 = jnp.int32
    return pl.pallas_call(
        functools.partial(prep_kernel, cap),
        out_shape=(
            jax.ShapeDtypeStruct((ROWS,), i32),
            jax.ShapeDtypeStruct((ROWS,), i32),
            jax.ShapeDtypeStruct((2 * ROWS,), i32),
            jax.ShapeDtypeStruct((4 * (cap + 1),), i32),
        ),
        in_specs=[SMEM] * 3,
        out_specs=(SMEM,) * 4,
        scratch_shapes=[pltpu.SMEM((ROWS * ROWS,), i32)],
    )(owner, sections, cols)


def iota(dim):
    return lax.broadcasted_iota(jnp.int32, (TILE, TILE), dim)


def picked(mask):
    return jnp.where(mask, 1.0, 0.0).astype(jnp.bfloat16)


def mm(a, b, dims=((1,), (0,))):
    return lax.dot_general(a, b, (dims, ((), ())), preferred_element_type=jnp.float32)


def counts_over(lists, owner, sections):
    cols = lists[...].reshape(TILE, TILE)
    line, lane = iota(0), iota(1)
    blocks = []
    for i in range(2):
        total = jnp.zeros((TILE, TILE), jnp.float32)
        for h in range(2):
            row = jnp.broadcast_to((owner[h : h + 1, :] >> 4).astype(jnp.float32), (TILE, TILE))
            choose = picked(lane + h * TILE == 2 * line + i)
            total = total + mm(choose, row.astype(jnp.bfloat16), ((1,), (1,)))
        blocks.append(total.astype(jnp.int32))
    mine = jnp.where(lane < BLOCK_COLS, blocks[0], blocks[1])
    sec0, sec1 = sections[0], sections[1]
    real = lane < 2 * BLOCK_COLS
    b = (lane & (BLOCK_COLS - 1)) >> 2
    rel = cols - b * BLOCK_COLS
    slab = picked(real & (rel >= 0) & (rel < SLAB) & ((mine == sec0) | (mine == sec1)))
    inner0 = (cols >= sec0 * ROWS) & (cols < sec0 * ROWS + ROWS)
    inner1 = (cols >= sec1 * ROWS) & (cols < sec1 * ROWS + ROWS)
    inner = picked(real & (inner0 | inner1))
    lane_b = (line & (BLOCK_COLS - 1)) >> 2
    to_y = picked((line < 2 * BLOCK_COLS) & ((lane_b >> 1) == lane))
    to_b = picked((line < 2 * BLOCK_COLS) & (lane_b == lane))
    per_y = mm(slab, to_y)
    per_b = mm(slab, to_b).astype(jnp.bfloat16)
    same_pair = picked(((line >> 4) == (lane >> 4)) & ((line & 1) == (lane & 1)))
    same_x = picked((line >> 5) == (lane >> 5))
    per_pair = mm(same_pair, per_b)
    per_x = mm(same_x, per_b)
    rows = jnp.zeros((TILE, TILE), jnp.float32)
    for i in range(2):
        own = picked((line >= i * BLOCK_COLS) & (line < (i + 1) * BLOCK_COLS))
        number = mm(inner, own).astype(jnp.bfloat16)
        rows = rows + mm(picked(blocks[i] == lane), number, ((0,), (0,)))
    over = per_y - FAST[0]
    over = jnp.maximum(over, rows - FAST[1])
    over = jnp.maximum(over, per_pair - FAST[2])
    over = jnp.maximum(over, per_x - FAST[3])
    return over


def spread_kernel(
    cap, tv, idx, owner, sections, send_row, picks,
    strips, cand, lists, over,
    left_out, left_in, right_out, row_out,
    s_idx, r_idx, s_left, r_left, s_right, r_right, s_core, r_core, s_list, r_list, s_row, r_row,
):
    r, c = lax.axis_index("row"), lax.axis_index("col")
    core, y, z = r % 2, c // 2, c % 2
    barrier = pltpu.get_barrier_semaphore()
    for d in range(1, COLS):
        pl.semaphore_signal(barrier, inc=1, device_id={"col": (c + d) % COLS}, device_id_type=MESH)
    for d in range(1, ROWS):
        pl.semaphore_signal(barrier, inc=1, device_id={"row": (r + d) % ROWS}, device_id_type=MESH)
    for i in range(2):
        for s in range(SECTIONS):
            source = sections[s] // 2
            for k in range(KB):
                for h in range(COLS):
                    left_out[h, i * ENTRIES + s * KB + k] = tv[
                        i * BLOCK_COLS + source * KB + k, h * STRIP : (h + 1) * STRIP, :
                    ]

    def pack(yd, _):
        for m in range(cap):
            right_out[yd, m] = tv[picks[yd * (cap + 1) + m]]
        return 0

    lax.fori_loop(0, 4, pack, 0)
    lists[r, c] = idx[...]
    left_in[c] = left_out[c]
    cand[core, y] = right_out[y]
    pl.semaphore_wait(barrier, COLS - 1 + ROWS - 1)

    idx_copies, left_copies, right_copies, core_copies = [], [], [], []
    for d in range(1, COLS):
        to = (c + d) % COLS
        copy = pltpu.make_async_remote_copy(
            idx, lists.at[r, c], s_idx.at[d], r_idx.at[d], device_id={"col": to}, device_id_type=MESH
        )
        copy.start()
        idx_copies.append(copy)
    for d in range(1, COLS):
        to = (c + d) % COLS
        copy = pltpu.make_async_remote_copy(
            left_out.at[to], left_in.at[c], s_left.at[d], r_left.at[d],
            device_id={"col": to}, device_id_type=MESH,
        )
        copy.start()
        left_copies.append(copy)
    for d in (2, 1, 3):
        to = (y + d) % 4
        copy = pltpu.make_async_remote_copy(
            right_out.at[to], cand.at[core, y], s_right.at[d], r_right.at[d],
            device_id={"col": to * 2 + z}, device_id_type=MESH,
        )
        copy.start()
        right_copies.append((d, copy))

    def to_core(src, origin, d):
        copy = pltpu.make_async_remote_copy(
            src, cand.at[core, origin], s_core.at[d], r_core.at[d],
            device_id={"row": r + 1 - 2 * core}, device_id_type=MESH,
        )
        copy.start()
        core_copies.append(copy)

    to_core(right_out.at[y], y, 0)
    for copy in idx_copies:
        copy.wait_recv()
    list_copies = []
    for d in range(1, ROWS):
        to = (r + d) % ROWS
        copy = pltpu.make_async_remote_copy(
            lists.at[r], lists.at[r], s_list.at[d], r_list.at[d],
            device_id={"row": to}, device_id_type=MESH,
        )
        copy.start()
        list_copies.append(copy)
    for copy in left_copies:
        copy.wait_recv()

    def reorder(t, _):
        j = send_row[t]
        for e in range(ENTRIES):
            row_out[t, e] = left_in[j // 2, (j % 2) * ENTRIES + e]
        return 0

    lax.fori_loop(0, ROWS, reorder, 0)
    strips[r] = row_out[r]
    row_copies = []
    for d in range(1, ROWS):
        to = (r + d) % ROWS
        copy = pltpu.make_async_remote_copy(
            row_out.at[to], strips.at[r], s_row.at[d], r_row.at[d],
            device_id={"row": to}, device_id_type=MESH,
        )
        copy.start()
        row_copies.append(copy)
    for copy in list_copies:
        copy.wait_recv()
    over[...] = counts_over(lists, owner, sections)
    for d, copy in right_copies:
        copy.wait_recv()
        origin = (y + 4 - d) % 4
        to_core(cand.at[core, origin], origin, d)
    for copy in row_copies + core_copies:
        copy.wait_recv()
    sent = [copy for _, copy in right_copies]
    for copy in idx_copies + left_copies + sent + core_copies + list_copies + row_copies:
        copy.wait_send()


def spread(cap, collective_id, tv, idx, owner, sections, send_row, picks):
    bf = jnp.bfloat16
    dma = pltpu.SemaphoreType.DMA
    return pl.pallas_call(
        functools.partial(spread_kernel, cap),
        out_shape=(
            jax.ShapeDtypeStruct((ROWS, ENTRIES, STRIP, TILE), bf),
            jax.ShapeDtypeStruct((2, 4, cap, TILE, TILE), bf),
            jax.ShapeDtypeStruct((ROWS, COLS, 1, TILE), jnp.int32),
            jax.ShapeDtypeStruct((TILE, TILE), jnp.float32),
        ),
        in_specs=[VMEM, VMEM, VMEM, SMEM, SMEM, SMEM],
        out_specs=(VMEM,) * 4,
        scratch_shapes=[
            pltpu.VMEM((COLS, 2 * ENTRIES, STRIP, TILE), bf),
            pltpu.VMEM((COLS, 2 * ENTRIES, STRIP, TILE), bf),
            pltpu.VMEM((4, cap, TILE, TILE), bf),
            pltpu.VMEM((ROWS, ENTRIES, STRIP, TILE), bf),
        ]
        + [dma((COLS,))] * 8
        + [dma((ROWS,))] * 4,
        compiler_params=params(20, collective_id=collective_id, has_side_effects=True),
    )(tv, idx, owner, sections, send_row, picks)


def lists_kernel(
    caps, lists, owner, sections, row_from, panel_from,
    keep_left, row_left, inner_left, here, there, keep, start, count, col_right, totals,
):
    cap_y, cap_left, cap_pair, cap_x = caps
    r, c = lax.axis_index("row"), lax.axis_index("col")
    x, zh = r >> 2, (r >> 1) & 1
    y, zl = c >> 1, c & 1
    secs = [sections[0], sections[1]]
    for m in range(cap_pair):
        here[m] = 0
        there[m] = 0
    for m in range(cap_x):
        keep[m] = 0

    def clear(m, _):
        for u in range(8):
            keep_left[m * 8 + u] = 0
        return 0

    lax.fori_loop(0, cap_left // 8, clear, 0)

    def left(g, n):
        j = row_from[g]
        line = g * COLS + (j >> 1)
        base = (j & 1) * BLOCK_COLS
        p = owner[g * ROWS + j] - r * ROWS
        for s in range(SECTIONS):
            for k in range(KB):
                rel = lists[line, base + (secs[s] >> 1) * KB + k] - secs[s] * ROWS
                keep_left[n] = g * ENTRIES + s * KB + k
                row_left[n] = p
                inner_left[n] = s * ROWS + rel
                n = n + ((rel >= 0) & (rel < ROWS)).astype(jnp.int32)
        return n

    totals[0] = lax.fori_loop(0, ROWS, left, jnp.int32(0))

    def ordered(g):
        a, b = panel_from[g], panel_from[ROWS + g]
        swap = (b < a).astype(jnp.int32)
        return ((swap, jnp.minimum(a, b)), (1 - swap, jnp.maximum(a, b)))

    def pairs(k2, carry):
        n_here, n_there = carry
        g = x * 4 + zh * 2 + k2
        used = jnp.int32(0)
        before = jnp.int32(-1)
        for s, j in ordered(g):
            source = j >> 1
            used = jnp.where(source == before, used, 0)
            before = source
            line = g * COLS + source
            base = (j & 1) * BLOCK_COLS
            near = (source & 1) == zl
            spot = k2 * 4 * cap_y + (source >> 1) * cap_y
            for z in range(2):
                mine = zl == z
                for k in range(KB):
                    b = y * 2 + z
                    rel = lists[line, base + b * KB + k] - b * BLOCK_COLS
                    ok = (rel >= 0) & (rel < SLAB)
                    take_here = (ok & near & mine).astype(jnp.int32)
                    take_there = (ok & near & jnp.logical_not(mine)).astype(jnp.int32)
                    at = jnp.minimum(spot + used, 8 * cap_y - 1)
                    here[n_here] = at
                    there[n_there] = at
                    n_here = n_here + take_here
                    n_there = n_there + take_there
                    used = used + ok.astype(jnp.int32)
        return n_here, n_there

    lax.fori_loop(0, 2, pairs, (jnp.int32(0), jnp.int32(0)))

    def per_x(xs, _):
        def per_zh(zs, n):
            def per_core(k2, carry):
                n, seen0, seen1 = carry
                g = xs * 4 + zs * 2 + k2
                for s, j in ordered(g):
                    source = j >> 1
                    sec = jnp.where(s == 0, secs[0], secs[1])
                    q = s * ROWS + owner[g * ROWS + j] - sec * ROWS
                    line = g * COLS + source
                    base = (j & 1) * BLOCK_COLS + c * KB
                    odd = source & 1
                    first = n
                    for k in range(KB):
                        rel = lists[line, base + k] - c * BLOCK_COLS
                        take = ((rel >= 0) & (rel < SLAB)).astype(jnp.int32)
                        seen = jnp.where(odd == 0, seen0, seen1)
                        at = jnp.minimum((zs * 2 + odd) * cap_pair + seen, 4 * cap_pair - 1)
                        col_right[xs * (cap_x + 1) + n] = rel
                        keep[jnp.where(xs == x, n, cap_x)] = at
                        n = n + take
                        seen0 = seen0 + take * (1 - odd)
                        seen1 = seen1 + take * odd
                    start[q] = xs * (cap_x + 1) + first
                    count[q] = n - first
                return n, seen0, seen1

            return lax.fori_loop(0, 2, per_core, (n, jnp.int32(0), jnp.int32(0)))[0]

        lax.fori_loop(0, 2, per_zh, jnp.int32(0))
        return 0

    lax.fori_loop(0, 4, per_x, 0)


def make_lists(caps, lists, owner, sections, row_from, panel_from):
    cap_y, cap_left, cap_pair, cap_x = caps
    more = cap_left + 8
    sizes = (more, more, more, cap_pair + 8, cap_pair + 8, cap_x + 8)
    sizes = sizes + (PANEL, PANEL, 4 * (cap_x + 1), 1)
    return pl.pallas_call(
        functools.partial(lists_kernel, caps),
        out_shape=tuple(jax.ShapeDtypeStruct((n,), jnp.int32) for n in sizes),
        in_specs=[SMEM] * 5,
        out_specs=(SMEM,) * len(sizes),
    )(lists, owner, sections, row_from, panel_from)


def gather_kernel(caps, strips, cand, keep_left, here, there, keep, left, right, held, other, send, recv):
    cap_y, cap_left, cap_pair, cap_x = caps
    r, c = lax.axis_index("row"), lax.axis_index("col")
    k = r % 2
    x, y = r // 4, c // 2
    me = ((r // 2) % 2) * 2 + c % 2
    cz = c + 1 - 2 * (c % 2)
    rz = (r // 4) * 4 + (r + 2) % 4
    cut = cap_left * 11 // 14
    zp, zh, zx = {"col": cz}, {"row": rz}, {"row": rz, "col": cz}
    yn, yb = {"col": (c + 2) % COLS}, {"col": (c + COLS - 2) % COLS}
    core = {"row": r + 1 - 2 * k}
    xn, xb = {"row": (r + 4) % ROWS}, {"row": (r + ROWS - 4) % ROWS}
    barrier = pltpu.get_barrier_semaphore()
    for peer in (zp, zh, zx, yn, yb, core, xn, xb):
        pl.semaphore_signal(barrier, inc=1, device_id=peer, device_id_type=MESH)
    half, part = cap_pair // 2, cap_x // 2

    for m in range(half):
        e = there[k * half + m]
        other[m] = cand[e // (4 * cap_y), (e // cap_y) % 4, e % cap_y]
    for m in range(cap_pair):
        e = here[m]
        held[me, m // half, m % half] = cand[e // (4 * cap_y), (e // cap_y) % 4, e % cap_y]

    def pack_left(m, _):
        for u in range(4):
            e = keep_left[m * 4 + u]
            left[c, m * 4 + u] = strips[e // ENTRIES, e % ENTRIES]
        return 0

    lax.fori_loop(0, cap_left // 4, pack_left, 0)
    pl.semaphore_wait(barrier, 8)

    started, done = [], []

    def push(src, dst, to):
        n = len(started)
        copy = pltpu.make_async_remote_copy(
            src, dst, send.at[n], recv.at[n], device_id=to, device_id_type=MESH
        )
        copy.start()
        started.append(copy)
        return copy

    def go(origin, a, b, to):
        piece = left.at[origin, pl.ds(a, b - a)]
        return push(piece, piece, to)

    def gx(origin, a, b, to):
        piece = right.at[origin, k, pl.ds(a, b - a)]
        return push(piece, piece, to)

    def arrived(copy):
        copy.wait_recv()
        done.append(copy)

    end = cap_left
    a_mid, b_mid = cut // 2, (cut + end) // 2
    c_m, c_p, c_o = (c + COLS - 2) % COLS, (c + 2) % COLS, (c + 4) % COLS
    z_m, z_p = (cz + COLS - 2) % COLS, (cz + 2) % COLS
    x_m, x_p, x_o = (x + 3) % 4, (x + 1) % 4, (x + 2) % 4
    z_of_p, z_of_h = (me // 2) * 2 + (me + 1) % 2, (me + 2) % 4
    z_of_x = (z_of_p + 2) % 4

    s1 = push(other, held.at[me, k], zp)
    s2 = push(other, held.at[me, k], zx)
    s3 = push(held.at[me, k], held.at[me, k], zh)
    k1 = go(c, 0, cut, zp)
    k2 = go(c, 0, cut, yn)
    k3 = go(c, 0, cut, yb)
    k10 = go(c, cut, end, yn)
    k11 = go(c, cut, end, yb)
    k12 = go(c, cut, end, zp)
    arrived(s1)
    t1 = push(held.at[z_of_p, k], held.at[z_of_p, k], core)
    arrived(s2)
    t2 = push(held.at[z_of_x, k], held.at[z_of_x, k], core)
    arrived(s3)
    t3 = push(held.at[z_of_h, k], held.at[z_of_h, k], core)
    arrived(k2)
    k6 = go(c_m, 0, a_mid, yn)
    arrived(k3)
    k7 = go(c_p, a_mid, cut, yb)
    arrived(k1)
    k4 = go(cz, 0, cut, yn)
    k5 = go(cz, 0, cut, yb)
    arrived(t1)
    arrived(t2)
    arrived(t3)
    for m in range(cap_x):
        e = keep[m]
        right[x, m // part, m % part] = held[e // cap_pair, (e // half) % 2, e % half]
    u1 = gx(x, 0, part, xn)
    u2 = gx(x, 0, part, xb)
    arrived(k10)
    k13 = go(c_m, cut, b_mid, yn)
    k14 = go(c_m, cut, end, zp)
    arrived(k11)
    k15 = go(c_p, b_mid, end, yb)
    k16 = go(c_p, cut, end, zp)
    arrived(u1)
    u3 = gx(x_m, 0, part // 2, xn)
    u4 = gx(x_m, 0, part, core)
    arrived(u2)
    u5 = gx(x_p, part // 2, part, xb)
    u6 = gx(x_p, 0, part, core)
    arrived(k4)
    k8 = go(z_m, 0, a_mid, yn)
    arrived(k5)
    k9 = go(z_p, a_mid, cut, yb)
    arrived(k13)
    k17 = go(c_o, cut, b_mid, zp)
    arrived(k15)
    k18 = go(c_o, b_mid, end, zp)
    arrived(u3)
    u7 = gx(x_o, 0, part // 2, core)
    arrived(u5)
    u8 = gx(x_o, part // 2, part, core)
    for copy in started:
        if not any(copy is seen for seen in done):
            copy.wait_recv()
    for copy in started:
        copy.wait_send()


COPIES = 32


def gather(caps, collective_id, strips, cand, keep_left, here, there, keep):
    cap_y, cap_left, cap_pair, cap_x = caps
    bf = jnp.bfloat16
    return pl.pallas_call(
        functools.partial(gather_kernel, caps),
        out_shape=(
            jax.ShapeDtypeStruct((COLS, cap_left, STRIP, TILE), bf),
            jax.ShapeDtypeStruct((4, 2, cap_x // 2, TILE, TILE), bf),
        ),
        in_specs=[VMEM, VMEM] + [SMEM] * 4,
        out_specs=(VMEM, VMEM),
        scratch_shapes=[
            pltpu.VMEM((4, 2, cap_pair // 2, TILE, TILE), bf),
            pltpu.VMEM((cap_pair // 2, TILE, TILE), bf),
        ]
        + [pltpu.SemaphoreType.DMA((COPIES,))] * 2,
        compiler_params=params(24, collective_id=collective_id, has_side_effects=True),
    )(strips, cand, keep_left, here, there, keep)


OUT_TILES = ROWS * SLAB
UNROLL = 4


def product_kernel(
    caps, left, right, row_left, inner_left, start, count, col_right, totals,
    squares, blank, out_of, touched_out, sums,
    acc, zeros, job_left, job_right, job_slot, job_first, slot_of, part, sem, zero_sem,
):
    cap_y, cap_left, cap_pair, cap_x = caps
    zeros[...] = jnp.zeros_like(zeros)
    for p in range(ROWS):
        pltpu.make_async_copy(zeros, blank.at[pl.ds(p * TILE, TILE)], zero_sem.at[p]).start()

    def clear(o, _):
        for u in range(16):
            slot_of[o * 16 + u] = -1
        return 0

    lax.fori_loop(0, OUT_TILES // 16, clear, 0)

    def per_left(m, carry):
        p, q = row_left[m], inner_left[m]
        place = start[q]

        def per_right(t, carry):
            n, touched = carry
            at = place + t
            xs = at // (cap_x + 1)
            o = p * SLAB + col_right[at]
            old = slot_of[o]
            fresh = old < 0
            slot = jnp.where(fresh, touched, old)
            job_left[n] = m
            job_right[n] = at - xs
            job_slot[n] = slot
            job_first[n] = fresh.astype(jnp.int32)
            slot_of[o] = slot
            out_of[slot] = o
            return n + 1, touched + fresh.astype(jnp.int32)

        return lax.fori_loop(0, count[q], per_right, carry)

    n, touched = lax.fori_loop(0, totals[0], per_left, (jnp.int32(0), jnp.int32(0)))
    touched_out[0] = touched
    for u in range(UNROLL):
        job_left[n + u] = 0
        job_right[n + u] = 0
        job_slot[n + u] = OUT_TILES
        job_first[n + u] = 1
    part_x = cap_x // 2

    def multiply(g, _):
        results = []
        for u in range(UNROLL):
            a = left[:, job_left[g * UNROLL + u]].reshape(TILE, TILE)
            e = job_right[g * UNROLL + u]
            b = right[e // cap_x, (e // part_x) % 2, e % part_x]
            results.append(jnp.dot(a, b, preferred_element_type=jnp.float32))
        for u in range(UNROLL):
            slot = job_slot[g * UNROLL + u]
            keep = (1 - job_first[g * UNROLL + u]).astype(jnp.float32)
            old = acc[slot]
            acc[slot] = results[u] + jnp.where(keep > 0, old, 0.0)
        return 0

    lax.fori_loop(0, (n + UNROLL - 1) // UNROLL, multiply, 0)
    part[...] = jnp.zeros_like(part)

    def finish(slot, _):
        value = acc[slot]
        value = value * value
        acc[slot] = value
        pltpu.make_async_copy(acc.at[slot], squares.at[slot], sem).start()
        col = lax.rem(out_of[slot], SLAB)
        part[col] += value.reshape(TILE // 8, 8, TILE).sum(axis=0)
        return 0

    lax.fori_loop(0, touched, finish, 0)
    sums[...] = part[...].sum(axis=1)

    def drain(slot, _):
        pltpu.make_async_copy(acc.at[slot], squares.at[slot], sem).wait()
        return 0

    lax.fori_loop(0, touched, drain, 0)
    for p in range(ROWS):
        pltpu.make_async_copy(zeros, blank.at[pl.ds(p * TILE, TILE)], zero_sem.at[p]).wait()


def products(caps, left, right, row_left, inner_left, start, count, col_right, totals):
    cap_y, cap_left, cap_pair, cap_x = caps
    jobs = cap_left * KB + UNROLL
    f32, i32 = jnp.float32, jnp.int32
    return pl.pallas_call(
        functools.partial(product_kernel, caps),
        out_shape=(
            jax.ShapeDtypeStruct((OUT_TILES, TILE, TILE), f32),
            jax.ShapeDtypeStruct((ROWS * TILE, SLAB * TILE), jnp.bfloat16),
            jax.ShapeDtypeStruct((OUT_TILES,), i32),
            jax.ShapeDtypeStruct((1,), i32),
            jax.ShapeDtypeStruct((ROWS, TILE), f32),
        ),
        in_specs=[VMEM, VMEM] + [SMEM] * 6,
        out_specs=(ANY, ANY, SMEM, SMEM, VMEM),
        scratch_shapes=[
            pltpu.VMEM((OUT_TILES + 1, TILE, TILE), f32),
            pltpu.VMEM((TILE, SLAB * TILE), jnp.bfloat16),
        ]
        + [pltpu.SMEM((jobs,), i32)] * 4
        + [
            pltpu.SMEM((OUT_TILES,), i32),
            pltpu.VMEM((ROWS, 8, TILE), f32),
            pltpu.SemaphoreType.DMA,
            pltpu.SemaphoreType.DMA((ROWS,)),
        ],
        compiler_params=params(30),
    )(left, right, row_left, inner_left, start, count, col_right, totals)


def total_kernel(mine, out, parts, send, recv):
    r = lax.axis_index("row")
    barrier = pltpu.get_barrier_semaphore()
    for d in range(1, ROWS):
        pl.semaphore_signal(barrier, inc=1, device_id={"row": (r + d) % ROWS}, device_id_type=MESH)
    parts[r] = mine[...]
    pl.semaphore_wait(barrier, ROWS - 1)
    copies = []
    for d in range(1, ROWS):
        copy = pltpu.make_async_remote_copy(
            mine, parts.at[r], send.at[d], recv.at[d],
            device_id={"row": (r + d) % ROWS}, device_id_type=MESH,
        )
        copy.start()
        copies.append(copy)
    for copy in copies:
        copy.wait_recv()
    out[...] = parts[...].sum(axis=0)
    for copy in copies:
        copy.wait_send()


def total(collective_id, mine):
    return pl.pallas_call(
        total_kernel,
        out_shape=jax.ShapeDtypeStruct((ROWS, TILE), jnp.float32),
        in_specs=[VMEM],
        out_specs=VMEM,
        scratch_shapes=[
            pltpu.VMEM((ROWS, ROWS, TILE), jnp.float32),
            pltpu.SemaphoreType.DMA((ROWS,)),
            pltpu.SemaphoreType.DMA((ROWS,)),
        ],
        compiler_params=params(4, collective_id=collective_id, has_side_effects=True),
    )(mine)


def write_kernel(squares, blank, out_of, touched_in, totals, out, tiles, block, factor, in_sem, out_sem):
    touched = touched_in[0]

    def fetch(slot, _):
        pltpu.make_async_copy(squares.at[slot], tiles.at[slot], in_sem.at[slot]).start()
        return 0

    lax.fori_loop(0, touched, fetch, 0)
    count = float(ROWS * ROWS * TILE)
    factor[...] = count / (totals[...] + 1e-06)

    def place(slot):
        o = out_of[slot]
        p = o // SLAB
        col = o - p * SLAB
        row = pl.ds(pl.multiple_of(p * TILE, TILE), TILE)
        lanes = pl.ds(pl.multiple_of(col * TILE, TILE), TILE)
        copy = pltpu.make_async_copy(block.at[slot], out.at[row, lanes], out_sem)
        return col, copy

    def scale(slot, _):
        pltpu.make_async_copy(squares.at[slot], tiles.at[slot], in_sem.at[slot]).wait()
        col, copy = place(slot)
        block[slot] = (tiles[slot] * factor[pl.ds(col, 1), :]).astype(jnp.bfloat16)
        copy.start()
        return 0

    lax.fori_loop(0, touched, scale, 0)

    def drain(slot, _):
        place(slot)[1].wait()
        return 0

    lax.fori_loop(0, touched, drain, 0)


def write(squares, blank, out_of, touched, totals):
    return pl.pallas_call(
        write_kernel,
        out_shape=jax.ShapeDtypeStruct((ROWS * TILE, SLAB * TILE), jnp.bfloat16),
        in_specs=[ANY, ANY, SMEM, SMEM, VMEM],
        out_specs=ANY,
        input_output_aliases={1: 0},
        scratch_shapes=[
            pltpu.VMEM((OUT_TILES, TILE, TILE), jnp.float32),
            pltpu.VMEM((OUT_TILES, TILE, TILE), jnp.bfloat16),
            pltpu.VMEM((ROWS, TILE), jnp.float32),
            pltpu.SemaphoreType.DMA((OUT_TILES,)),
            pltpu.SemaphoreType.DMA,
        ],
        compiler_params=params(24),
    )(squares, blank, out_of, touched, totals)


def per_device(tile_values, tile_columns, owner_map, section_rows):
    flat = tile_columns.reshape(-1)
    idx = jnp.pad(flat, (0, TILE - flat.shape[0])).reshape(1, TILE)
    tv = tile_values.reshape(2 * COLS * KB, TILE, TILE)
    owner_rows = owner_map.reshape(2, TILE)

    def first(caps, collective_id):
        send_row, row_from, panel_from, picks = prep(caps[0], owner_map, section_rows, flat)
        got = spread(caps[0], collective_id, tv, idx, owner_rows, section_rows, send_row, picks)
        return *got, row_from, panel_from

    def rest(caps, ids, strips, cand, lists, over, row_from, panel_from):
        made = make_lists(
            caps, lists.reshape(ROWS * COLS, TILE), owner_map, section_rows, row_from, panel_from
        )
        keep_left, row_left, inner_left, here, there, keep, start, count, col_right, totals = made
        left, right = gather(caps, ids[0], strips, cand, keep_left, here, there, keep)
        squares, blank, out_of, touched, sums = products(
            caps, left, right, row_left, inner_left, start, count, col_right, totals
        )
        return write(squares, blank, out_of, touched, total(ids[1], sums))

    got = first(FAST, 0)
    return lax.cond(
        jnp.max(got[3]) > 0,
        lambda *_: rest(FULL, (4, 5), *first(FULL, 3)),
        lambda *args: rest(FAST, (1, 2), *args),
        *got,
    )


def solution(mesh):
    both = ("row", "col")
    in_specs = (P(both, None, None, None, None), P(both, None, None), P(), P())
    return jax.shard_map(
        per_device, mesh=mesh, in_specs=in_specs, out_specs=P("row", "col"), check_vma=False
    )
```

time: 125 us -> 107 us (0.86)
  Pallas kernels: 114 us -> 97.6 us
  local copies, waits for them, and re-layouts: 3.58 us -> 7.77 us
  other arithmetic: 4.43 us -> 0.62 us
  between operations: 3.42 us -> 0.69 us
    pallas_call x1, Pallas kernels: 42.3 us -> 33.1 us  [spread(): pl.pallas_call(functools.partial(spread_kernel, cap), out_shape=(jax.Shap...]
    cond x0 -> x18, local copies, waits for them, and re-layouts: none -> 5.67 us
    pallas_call x1, Pallas kernels: 6.51 us -> 2.06 us  [prep(): pl.pallas_call(functools.partial(prep_kernel, cap), out_shape=(jax.ShapeD...]
    pallas_call x1, Pallas kernels: 31.8 us -> 29.4 us  [gather(): pl.pallas_call(functools.partial(gather_kernel, caps), out_shape=(jax.Sha...]
    or x1 -> x0, other arithmetic: 2.03 us -> none  [overflow(): panel = (block == sections[0]) | (block == sections[1])]
    slice x2 -> x0, local copies, waits for them, and re-layouts: 1.64 us -> none  [the longest x1 1.47 us: overflow(): panel = (block == sections[0]) | (block == sections[1])]
    reduce_max x3 -> x1, other arithmetic: 1.92 us -> 0.62 us  [per_device(): jnp.max(got[3]) > 0]
where the time goes in v2:
time: 107 us
  Pallas kernels  97.6 us (91%)
  local copies, waits for them, and re-layouts  7.77 us (7%)
    pallas_call x1, Pallas kernels, spread(): pl.pallas_call(functools.partial(spread_kernel, cap), out_shape=(jax.Shap...  33.1 us
    pallas_call x1, Pallas kernels, gather(): pl.pallas_call(functools.partial(gather_kernel, caps), out_shape=(jax.Sha...  29.4 us
    pallas_call x1, Pallas kernels, products(): pl.pallas_call(functools.partial(product_kernel, caps), out_shape=(jax.Sh...  10.8 us
    pallas_call x1, Pallas kernels, total(): pl.pallas_call(total_kernel, out_shape=jax.ShapeDtypeStruct((ROWS, TILE),...  8.49 us
    pallas_call x1, Pallas kernels, write(): pl.pallas_call(write_kernel, out_shape=jax.ShapeDtypeStruct((ROWS * TILE,...  8.32 us
    cond x18, local copies, waits for them, and re-layouts  5.67 us
    pallas_call x1, Pallas kernels, make_lists(): pl.pallas_call(functools.partial(lists_kernel, caps), out_shape=tuple((ja...  5.32 us

profile of v2, /device:TPU:1, one launch (start us, length us, event | category | flops | bytes accessed | tf_op | source)
XLA Modules:
  0.0 106.7 jit_solution(14732997209671348304)
XLA Ops:
  0.0 0.8 copy.11
  0.8 0.1 reshape.19.cols
  0.9 2.1 %shard_map.48 = (s32[16]{0:T(128)}, s32[16]{0:T(128)S(1)}, s32[32]{0:T(128)S(1)}, s32[36]{0:T(128)}) custom-call(s32[256]{0:T(256)} %owner.1, s32[2]{0:T(128)} %sections.3, s32[64]{0:T(128)S(1)} %reshape.19.cols), custom_call_target="tpu_custom_call" | custom-call | tf_op jit(solution)/shard_map/pallas_call | solution.py:74
  2.9 0.0 copy-start.21
  2.9 0.6 copy-done.21
  3.6 0.6 copy-done.22
  4.2 33.1 %shard_map.49 = (bf16[16,8,16,128]{3,2,1,0:T(8,128)(2,1)S(1)}, bf16[2,4,8,128,128]{4,3,2,1,0:T(8,128)(2,1)S(1)}, s32[16,8,1,128]{3,2,1,0:T(1,128)S(1)}, f32[128,128]{1,0:T(8,128)S(1)}) custom-call(bf16[64,128,128]{2,1,0:T(8,128)(2,1)} %bitcast.9, s32[1,128]{1,0:T(1,128)S(1)} %pad_bitcast_fusion.idx, s32[2,128]{1,0:T(2,128)} %bitcast.12, s32[2]{0:T(128)} %sections.3, ...), custom_call_target="tpu_custom_call" | custom-call | tf_op jit(solution)/shard_map/pallas_call | solution.py:256
  37.3 0.6 reduce_max.9
  38.6 68.1 %conditional.1 = (bf16[2048,1536]{1,0:T(8,128)(2,1)}) conditional(s32[]{:T(128)} %convert_element_type.3, (s32[16,8,1,128]{3,2,1,0:T(1,128)S(1)}, s32[256]{0:T(256)}, s32[2]{0:T(128)}, s32[16]{0:T(128)S(1)}, s32[32]{0:T(128)S(1)}, /*index=5*/bf16[16,8,16,128]{3,2,1,0:T(8,128)(2,1)S(1)}, bf16[2,4,8,128,128]{4,3,2,1,0:T(8,128)(2,1)S(1)}) %tuple.11, ...), branch_computations={%region_1.2_spmd, %region_2.3_spmd} | conditional | bytes 33829392 | solution.py:783
  38.6 5.3 %branch_0_fun.5 = (s32[64]{0:T(128)}, s32[64]{0:T(128)}, s32[64]{0:T(128)}, s32[18]{0:T(128)}, s32[18]{0:T(128)}, /*index=5*/s32[24]{0:T(128)}, s32[32]{0:T(128)}, s32[32]{0:T(128)}, s32[68]{0:T(128)}, s32[1]{0:T(128)}) custom-call(s32[128,128]{1,0:T(8,128)S(1)} %bitcast.11, s32[256]{0:T(256)} %get-tuple-element.37.owner, s32[2]{0:T(128)} %get-tuple-element.38.sections, ...), custom_call_target="tpu_custom_call" | custom-call | tf_op jit(solution)/shard_map/cond/branch_0_fun/pallas_call | solution.py:392
  43.9 0.0 copy-start.17
  43.9 0.6 copy-done.17
  44.6 0.6 copy-done.18
  45.2 0.6 copy-done.19
  45.8 0.7 copy-done.20
  46.4 29.4 %branch_0_fun.6 = (bf16[8,56,16,128]{3,2,1,0:T(8,128)(2,1)S(1)}, bf16[4,2,8,128,128]{4,3,2,1,0:T(8,128)(2,1)S(1)}) custom-call(bf16[16,8,16,128]{3,2,1,0:T(8,128)(2,1)S(1)} %get-tuple-element.34.strips, bf16[2,4,8,128,128]{4,3,2,1,0:T(8,128)(2,1)S(1)} %get-tuple-element.35.cand, s32[64]{0:T(128)S(1)} %copy-done.17, s32[18]{0:T(128)S(1)} %copy-done.18, ...), custom_call_target="tpu_custom_call" | custom-call | tf_op jit(solution)/shard_map/cond/branch_0_fun/pallas_call | solution.py:532
  75.9 0.7 copy-done.9
  76.6 0.7 copy-done.10
  77.2 0.6 copy-done.11
  77.9 0.6 copy-done.12
  78.5 0.6 copy-done.13
  79.1 10.8 %branch_0_fun.7 = (f32[192,128,128]{2,1,0:T(8,128)S(1)}, bf16[2048,1536]{1,0:T(8,128)(2,1)}, s32[192]{0:T(256)S(1)}, s32[1]{0:T(128)}, f32[16,128]{1,0:T(8,128)S(1)}) custom-call(bf16[8,56,16,128]{3,2,1,0:T(8,128)(2,1)S(1)} %get-tuple-element.45.left, bf16[4,2,8,128,128]{4,3,2,1,0:T(8,128)(2,1)S(1)} %get-tuple-element.46.right, s32[64]{0:T(128)S(1)} %copy-done.9, ...), custom_call_target="tpu_custom_call" | custom-call | tf_op jit(solution)/shard_map/cond/branch_0_fun/pallas_call | solution.py:643
  89.9 8.5 %branch_0_fun.8.totals = f32[16,128]{1,0:T(8,128)S(1)} custom-call(f32[16,128]{1,0:T(8,128)S(1)} %get-tuple-element.57.mine), custom_call_target="tpu_custom_call" | custom-call | tf_op jit(solution)/shard_map/cond/branch_0_fun/pallas_call | solution.py:692
  98.4 8.3 %branch_0_fun.9 = bf16[2048,1536]{1,0:T(8,128)(2,1)} custom-call(f32[192,128,128]{2,1,0:T(8,128)S(1)} %get-tuple-element.53.squares, bf16[2048,1536]{1,0:T(8,128)(2,1)} %get-tuple-element.54.blank, s32[192]{0:T(256)S(1)} %get-tuple-element.55.out_of, s32[1]{0:T(128)} %get-tuple-element.56.touched_in, ...), custom_call_target="tpu_custom_call", output_to_operand_aliasing={{}: (1, {})} | custom-call | tf_op jit(solution)/shard_map/cond/branch_0_fun/pallas_call | solution.py:743
  (10 shorter events, 0.0 us)
Async XLA Ops:
  2.9 0.7 copy-start.21
  3.6 0.6 copy-start.22
  43.9 0.7 copy-start.17
  44.6 0.6 copy-start.18
  45.2 0.6 copy-start.19
  45.8 0.7 copy-start.20
  75.9 0.7 copy-start.9
  76.6 0.7 copy-start.10
  77.2 0.6 copy-start.11
  77.8 0.6 copy-start.12
  78.5 0.6 copy-start.13
